TPU v7x, 128 devices: a whole 4x4x4 slice. The times are simulated.
128 devices in a mesh: section: 2 (over x_hi), dp: 4 (over x_lo, core), tensor: 16 (over z, y).
Axes of the slice: x: 4 (x_hi: 2, x_lo: 2; x = x_hi * 2 + x_lo), y: 4, z: 4, core: 2. Of those that a mesh axis runs over, the one named last changes fastest.
Arguments:
- incoming: bfloat16 [2, 3, 1024, 8192], P('section', None, ('dp', 'tensor')), may hold values from -6 to 6
- hidden: bfloat16 [2, 3, 1024, 8192], P('section', None, ('dp', 'tensor')), may hold values from -6 to 6
- expert_out: bfloat16 [2, 3, 1024, 2, 8192], P('section', None, ('dp', 'tensor')), may hold values from -0.59765625 to 0.59765625
- routes: int32 [2, 3, 1024, 2], P('section', None, ('dp', 'tensor')), may hold values from 0 to 15, all different within a row; in each aligned block of 16 rows (0 to 15, 16 to 31, ..., all dimensions but the last counted through in order) at most 4 rows name the same one
- expert_back: bfloat16 [2, 3, 4096, 8192], P('section', None, ('dp', 'tensor')), may hold values from -0.59765625 to 0.59765625
- scan_out: bfloat16 [2, 3, 1024, 8192], P('section', None, 'dp', 'tensor'), may hold values from -6 to 6
- gate_in: bfloat16 [2, 3, 1024, 8192], P('section', None, 'dp', 'tensor'), may hold values from -9 to 9
- w_out: bfloat16 [2, 8192, 8192], P('section', 'tensor'), may hold values from -0.0625 to 0.0625
- w_router: bfloat16 [2, 8192, 16], P('section', 'dp'), may hold values from -0.0625 to 0.0625
- norm_gain: bfloat16 [2, 8192], P('section', 'dp'), may hold values from 0.5 to 1.5
Outputs:
- passed: bfloat16 [2, 3, 1024, 8192], P('section', None, ('dp', 'tensor'))
- scan_grad: bfloat16 [2, 3, 1024, 8192], P('section', None, 'dp', 'tensor')
- gate_grad: bfloat16 [2, 3, 1024, 8192], P('section', None, 'dp', 'tensor')
- expert_grad: bfloat16 [2, 3, 4096, 8192], P('section', None, ('dp', 'tensor'))
- w_out_grad: float32 [2, 8192, 8192], P('section', 'tensor', 'dp')
- router_grad: float32 [2, 8192, 16], P('section', 'dp')
- gain_grad: float32 [2, 8192], P('section', 'dp')
Inputs may be any that keep to these rules, and one draw needn't show every extreme that they name: `routes`: each row names 2 different experts. In each aligned block of 16 rows (the rows of one device) no expert is named by more than 4 rows, a bound that some block reaches.
All inputs are finite; a program needn't handle non-finite values.
Results may differ from a plain program's by a relative error of at most 0.025.
Values may be sent and summed in bfloat16 or wider, within the bound.
A program may use at most 192 MiB of HBM per device.

v0:
```python
import jax
import jax.numpy as jnp
from jax import lax
from jax.experimental import pallas as pl
from jax.experimental.pallas import tpu as pltpu
from jax.sharding import PartitionSpec as P

MESH = pl.DeviceIdType.MESH
CHUNKS = 8
QCOL = 256
CCOL = 1024
HALF = 512


def mixer_kernel(
    passed_ref, scan_ref, gate_ref, w_hbm,
    scan_out, gate_out, wgrad_out,
    G, W, gT, inner, own, outv, msend, mrecv, xsend, xrecv, stage,
    ag_s, ag_r, w_sem, ms_s, ms_r, xs_s, xs_r, out_sem, fin_sem,
):
    d = lax.axis_index("dp")
    tau = lax.axis_index("tensor")
    z = tau // 4
    y = tau % 4
    core = d % 2
    xl = d // 2
    mate = xl * 2 + (1 - core)
    xnbr = (1 - xl) * 2 + core

    def at_y(k):
        return z * 4 + (y + k) % 4

    def at_z(k):
        return ((z + k) % 4) * 4 + y

    barrier = pltpu.get_barrier_semaphore()
    for peer in (at_y(1), at_y(3), at_z(1), at_z(3)):
        pl.semaphore_signal(barrier, inc=1, device_id={"tensor": peer}, device_id_type=MESH)
    for peer in (mate, xnbr):
        pl.semaphore_signal(barrier, inc=1, device_id={"dp": peer}, device_id_type=MESH)

    def w_load(c, carry):
        for q in range(4):
            pltpu.make_async_copy(
                w_hbm.at[:, pl.ds(pl.multiple_of(q * 2048 + c * QCOL, QCOL), QCOL)],
                W.at[c, :, pl.ds(q * QCOL, QCOL)],
                w_sem.at[c],
            ).start()
        return carry

    for c in range(CHUNKS):
        for t in range(3):
            for q in range(4):
                G[c, t, z, pl.ds(pl.multiple_of(16 * y, 16), 16), q * QCOL : (q + 1) * QCOL] = (
                    passed_ref[t, :, q * 2048 + c * QCOL : q * 2048 + (c + 1) * QCOL]
                )
    pl.semaphore_wait(barrier, 6)

    def y16(k):
        return pl.ds(pl.multiple_of(16 * ((y + k) % 4), 16), 16)

    def shard(c, h, k, c0, cw):
        if h == 0:
            return G.at[c, :, z, y16(k), pl.ds(h * HALF + c0, cw)]
        return G.at[c, :, (z + k) % 4, y16(0), pl.ds(h * HALF + c0, cw)]

    def block(c, h, k, c0, cw):
        if h == 0:
            return G.at[c, :, (z + k) % 4, :, pl.ds(h * HALF + c0, cw)]
        return G.at[c, :, :, y16(k), pl.ds(h * HALF + c0, cw)]

    def nbr(h, stage_no, step):
        return at_y(step) if (h == 0) == (stage_no == 0) else at_z(step)

    def region(c, h, kind, k):
        fn = shard if kind < 4 else block
        if kind % 4 < 2:
            return fn(c, h, k, 0, HALF)
        return fn(c, h, k, (kind % 2) * (HALF // 2), HALF // 2)

    def ag_copy(c, h, kind, k):
        ref = region(c, h, kind, k)
        return pltpu.make_async_remote_copy(
            src_ref=ref, dst_ref=ref, send_sem=ag_s.at[c, h, kind], recv_sem=ag_r.at[c, h, kind],
            device_id={"tensor": nbr(h, kind // 4, 1 if kind % 2 == 0 else 3)}, device_id_type=MESH,
        )

    def send(c, h, kind):
        step = 0 if kind % 4 < 2 else (3 if kind % 2 == 0 else 1)
        ag_copy(c, h, kind, step).start()

    def recv(c, h, kind):
        step = (3 if kind % 2 == 0 else 1) if kind % 4 < 2 else 2
        ag_copy(c, h, kind, step).wait_recv()

    def t0(c):
        for h in range(2):
            send(c, h, 0)
            send(c, h, 1)

    def t1(c):
        for h in range(2):
            recv(c, h, 0)
            send(c, h, 2)
            recv(c, h, 1)
            send(c, h, 3)

    def t2(c):
        for h in range(2):
            recv(c, h, 2)
            recv(c, h, 3)
            send(c, h, 4)
            send(c, h, 5)

    def t3(c):
        for h in range(2):
            recv(c, h, 4)
            send(c, h, 6)
            recv(c, h, 5)
            send(c, h, 7)

    def mate_copy(c):
        return pltpu.make_async_remote_copy(
            src_ref=msend.at[c % 2], dst_ref=mrecv.at[c], send_sem=ms_s.at[c], recv_sem=ms_r.at[c],
            device_id={"dp": mate}, device_id_type=MESH,
        )

    def x_copy(c):
        return pltpu.make_async_remote_copy(
            src_ref=xsend.at[c % 2], dst_ref=xrecv.at[c], send_sem=xs_s.at[c], recv_sem=xs_r.at[c],
            device_id={"dp": xnbr}, device_id_type=MESH,
        )

    def out_copy(c):
        return pltpu.make_async_copy(
            outv.at[c], wgrad_out.at[:, pl.ds(pl.multiple_of(c * QCOL, QCOL), QCOL)], out_sem.at[c]
        )

    def t4(c):
        for h in range(2):
            recv(c, h, 6)
            recv(c, h, 7)
        pltpu.make_async_copy(W.at[c], W.at[c], w_sem.at[c]).wait()
        for t in range(3):
            rows = G[c, t].reshape(256, CCOL)
            inner[t] += lax.dot_general(
                rows, W[c], (((1,), (1,)), ((), ())), preferred_element_type=jnp.float32
            )

        @pl.when(c >= 2)
        def _():
            mate_copy(c - 2).wait_send()

        for cq in range(2):
            for xq in range(2):
                q = xq * 2 + cq
                cols = slice(q * QCOL, (q + 1) * QCOL)
                part = jnp.zeros((512, QCOL), jnp.float32)
                for t in range(3):
                    part += jnp.dot(
                        gT[:, t * 256 : (t + 1) * 256],
                        G[c, t, :, :, cols].reshape(256, QCOL),
                        preferred_element_type=jnp.float32,
                    )

                @pl.when(core == cq)
                def _():
                    own[c % 2, xq] = part

                @pl.when(core != cq)
                def _():
                    msend[c % 2, xq] = part.astype(jnp.bfloat16)

        mate_copy(c).start()

    def r1(c):
        mate_copy(c).wait_recv()

        @pl.when(c >= 2)
        def _():
            x_copy(c - 2).wait_send()

        xsend[c % 2] = (own[c % 2, 1 - xl] + mrecv[c, 1 - xl].astype(jnp.float32)).astype(jnp.bfloat16)
        x_copy(c).start()
        outv[c] = own[c % 2, xl] + mrecv[c, xl].astype(jnp.float32)

    def r2(c):
        x_copy(c).wait_recv()
        outv[c] += xrecv[c].astype(jnp.float32)
        out_copy(c).start()

    t0(0)
    lax.fori_loop(0, CHUNKS, w_load, 0)
    for t in range(3):
        gate_f = gate_ref[t].astype(jnp.float32)
        gated = scan_ref[t].astype(jnp.float32) * gate_f * jax.nn.sigmoid(gate_f)
        gT[:, t * 256 : (t + 1) * 256] = gated.T.astype(jnp.bfloat16)
    inner[...] = jnp.zeros_like(inner)

    def step(s, carry):
        for lag, fn in ((0, t0), (3, t3), (2, t2), (1, t1), (5, r1), (6, r2), (4, t4)):
            low = lag + (1 if fn is t0 else 0)

            @pl.when((s >= low) & (s < CHUNKS + lag))
            def _():
                fn(s - lag)

        return carry

    lax.fori_loop(0, CHUNKS + 7, step, 0)

    for t in range(3):
        gate_f = gate_ref[t].astype(jnp.float32)
        sig = jax.nn.sigmoid(gate_f)
        rows = inner[t]
        stage[0, t] = (rows * gate_f * sig).astype(jnp.bfloat16)
        stage[1, t] = (
            rows * scan_ref[t].astype(jnp.float32) * sig * (1.0 + gate_f * (1.0 - sig))
        ).astype(jnp.bfloat16)
    fin = [
        pltpu.make_async_copy(stage.at[0], scan_out, fin_sem.at[0]),
        pltpu.make_async_copy(stage.at[1], gate_out, fin_sem.at[1]),
    ]
    for cp in fin:
        cp.start()

    def drain(c, carry):
        for h in range(2):
            for kind in range(8):
                ag_copy(c, h, kind, 0 if kind % 4 < 2 else (3 if kind % 2 == 0 else 1)).wait_send()
        out_copy(c).wait()
        return carry

    lax.fori_loop(0, CHUNKS, drain, 0)
    for c in (CHUNKS - 2, CHUNKS - 1):
        mate_copy(c).wait_send()
        x_copy(c).wait_send()
    for cp in fin:
        cp.wait()


def mixer(passed, scan, gate, weight):
    bf16, f32 = jnp.bfloat16, jnp.float32
    vmem = pl.BlockSpec(memory_space=pltpu.VMEM)
    hbm = pl.BlockSpec(memory_space=pl.ANY)
    return pl.pallas_call(
        mixer_kernel,
        out_shape=(
            jax.ShapeDtypeStruct((3, 256, 512), bf16),
            jax.ShapeDtypeStruct((3, 256, 512), bf16),
            jax.ShapeDtypeStruct((512, 2048), f32),
        ),
        in_specs=[vmem, vmem, vmem, hbm],
        out_specs=(hbm, hbm, hbm),
        scratch_shapes=[
            pltpu.VMEM((CHUNKS, 3, 4, 64, CCOL), bf16),
            pltpu.VMEM((CHUNKS, 512, CCOL), bf16),
            pltpu.VMEM((512, 768), bf16),
            pltpu.VMEM((3, 256, 512), f32),
            pltpu.VMEM((2, 2, 512, QCOL), f32),
            pltpu.VMEM((CHUNKS, 512, QCOL), f32),
            pltpu.VMEM((2, 2, 512, QCOL), bf16),
            pltpu.VMEM((CHUNKS, 2, 512, QCOL), bf16),
            pltpu.VMEM((2, 512, QCOL), bf16),
            pltpu.VMEM((CHUNKS, 512, QCOL), bf16),
            pltpu.VMEM((2, 3, 256, 512), bf16),
            pltpu.SemaphoreType.DMA((CHUNKS, 2, 8)),
            pltpu.SemaphoreType.DMA((CHUNKS, 2, 8)),
            pltpu.SemaphoreType.DMA((CHUNKS,)),
            pltpu.SemaphoreType.DMA((CHUNKS,)),
            pltpu.SemaphoreType.DMA((CHUNKS,)),
            pltpu.SemaphoreType.DMA((CHUNKS,)),
            pltpu.SemaphoreType.DMA((CHUNKS,)),
            pltpu.SemaphoreType.DMA((CHUNKS,)),
            pltpu.SemaphoreType.DMA((2,)),
        ],
        compiler_params=pltpu.CompilerParams(
            collective_id=0, has_side_effects=True, vmem_limit_bytes=60 * 1024 * 1024
        ),
        cost_estimate=pl.CostEstimate(flops=13_000_000_000, bytes_accessed=30_000_000, transcendentals=0),
    )(passed, scan, gate, weight)


def passed_along(shard, axis, by):
    length = lax.axis_size(axis)
    pairs = [(i, i + by) for i in range(length) if 0 <= i + by < length]
    return lax.ppermute(shard, axis, pairs)


def slot_rows(expert_ids, experts, capacity):
    flat_ids = expert_ids.reshape(-1)
    onehot = (flat_ids[:, None] == jnp.arange(experts, dtype=jnp.int32)[None, :]).astype(jnp.int32)
    before = jnp.cumsum(onehot, axis=0, dtype=jnp.int32) - onehot
    slot_index = jnp.sum(before * onehot, axis=1, dtype=jnp.int32)
    return flat_ids * capacity + slot_index


def on_device(
    incoming, hidden, expert_out, routes, expert_back, scan_out, gate_in, w_out, w_router, norm_gain
):
    micro_count = incoming.shape[1]
    tok_rows = incoming.shape[2]
    model_width = incoming.shape[3]
    top_count = routes.shape[3]
    experts = w_router.shape[2]
    tensor_size = lax.axis_size("tensor")
    capacity = expert_back.shape[2] // tensor_size
    inner_width = scan_out.shape[3]
    weight_rows = w_out[0]
    section_id = lax.axis_index("section")
    router_full, gain_full = (
        lax.all_gather(w_router[0], "dp", axis=0, tiled=True),
        lax.all_gather(norm_gain[0], "dp", axis=0, tiled=True),
    )
    gain_f = gain_full.astype(jnp.float32)
    expert_range = jnp.arange(experts, dtype=jnp.int32)
    router_acc = jnp.zeros((model_width, experts), jnp.float32)
    gain_acc = jnp.zeros((model_width,), jnp.float32)
    passed_list = []
    expert_list = []
    received = incoming[0, 0]
    for micro_step in range(micro_count):
        upstream = incoming[0, micro_step]
        if micro_step > 0:
            upstream = jnp.where(section_id == 1, upstream, received)
        returned = lax.all_to_all(
            expert_back[0, micro_step], "tensor", split_axis=0, concat_axis=0, tiled=True
        )
        hidden_f = hidden[0, micro_step].astype(jnp.float32)
        inv_rms = 1.0 / jnp.sqrt(jnp.mean(hidden_f * hidden_f, axis=1, keepdims=True) + 1e-05)
        normed = (hidden_f * inv_rms * gain_f).astype(jnp.bfloat16)
        logits = jnp.dot(normed, router_full, preferred_element_type=jnp.float32)
        weights = jnp.exp(logits)
        route_probs = weights / jnp.sum(weights, axis=1, keepdims=True)
        expert_ids = routes[0, micro_step]
        chosen = (expert_ids[:, :, None] == expert_range[None, None, :]).astype(jnp.float32)
        route_prob = jnp.sum(chosen * route_probs[:, None, :], axis=2)
        score_grad = jnp.einsum(
            "td,tkd->tk", upstream, expert_out[0, micro_step], preferred_element_type=jnp.float32
        )
        prob_grad = jnp.sum(chosen * score_grad[:, :, None], axis=1)
        logit_grad = (
            route_probs * (prob_grad - jnp.sum(route_probs * prob_grad, axis=1, keepdims=True))
        ).astype(jnp.bfloat16)
        row_index = slot_rows(expert_ids, experts, capacity)
        back_rows = (
            returned[row_index].astype(jnp.float32).reshape(tok_rows, top_count, model_width)
        )
        router_back = lax.dot_general(
            logit_grad, router_full, (((1,), (1,)), ((), ())), preferred_element_type=jnp.float32
        )
        norm_grad = router_back + jnp.sum(back_rows, axis=1)
        scaled = norm_grad * gain_f
        hidden_grad = inv_rms * scaled - hidden_f * inv_rms**3 * jnp.mean(
            scaled * hidden_f, axis=1, keepdims=True
        )
        upstream_f = upstream.astype(jnp.float32)
        passed = (upstream_f + hidden_grad).astype(jnp.bfloat16)
        if micro_step + 1 < micro_count:
            received = passed_along(passed, "section", -1)
        gain_acc = gain_acc + jnp.sum(norm_grad * hidden_f * inv_rms, axis=0)
        router_acc = router_acc + lax.dot_general(
            normed, logit_grad, (((0,), (0,)), ((), ())), preferred_element_type=jnp.float32
        )
        sent = (
            (route_prob[:, :, None] * upstream_f[:, None, :])
            .astype(jnp.bfloat16)
            .reshape(tok_rows * top_count, model_width)
        )
        send_buffer = (
            jnp.zeros((experts * capacity, model_width), jnp.bfloat16).at[row_index].set(sent)
        )
        dispatched = lax.all_to_all(send_buffer, "tensor", split_axis=0, concat_axis=0, tiled=True)
        passed_list.append(passed)
        expert_list.append(dispatched)
    passed_all = jnp.stack(passed_list)
    scan_grad, gate_grad, weight_grad = mixer(passed_all, scan_out[0], gate_in[0], weight_rows)
    summed = (
        lax.psum(router_acc.astype(jnp.bfloat16), "tensor").astype(jnp.float32),
        lax.psum(gain_acc.astype(jnp.bfloat16), "tensor").astype(jnp.float32),
    )
    router_part, gain_part = (
        lax.psum_scatter(
            summed[0].astype(jnp.bfloat16), "dp", scatter_dimension=0, tiled=True
        ).astype(jnp.float32),
        lax.psum_scatter(
            summed[1].astype(jnp.bfloat16), "dp", scatter_dimension=0, tiled=True
        ).astype(jnp.float32),
    )
    return (
        passed_all[None],
        scan_grad[None],
        gate_grad[None],
        jnp.stack(expert_list)[None],
        weight_grad[None],
        router_part[None],
        gain_part[None],
    )


def solution(mesh):
    placed = (
        P("section", None, ("dp", "tensor"), None),
        P("section", None, ("dp", "tensor"), None),
        P("section", None, ("dp", "tensor"), None, None),
        P("section", None, ("dp", "tensor"), None),
        P("section", None, ("dp", "tensor"), None),
        P("section", None, "dp", "tensor"),
        P("section", None, "dp", "tensor"),
        P("section", "tensor", None),
        P("section", "dp", None),
        P("section", "dp"),
    )
    return jax.shard_map(
        on_device,
        mesh=mesh,
        in_specs=placed,
        out_specs=(
            P("section", None, ("dp", "tensor"), None),
            P("section", None, "dp", "tensor"),
            P("section", None, "dp", "tensor"),
            P("section", None, ("dp", "tensor"), None),
            P("section", "tensor", "dp"),
            P("section", "dp", None),
            P("section", "dp"),
        ),
        check_vma=False,
    )
```

profile of v0, /device:TPU:1, one launch (start us, length us, event | category | flops | bytes accessed | tf_op | source)
XLA Modules:
  0.0 367.9 jit_solution(7096385737649090756)
XLA Ops:
  7.2 3.1 fusion.67
  10.3 1.2 all_to_all.42
  11.5 8.6 %all-to-all-start = ((bf16[16,4,8192]{2,1,0:T(4,128)(2,1)}), bf16[16,4,8192]{2,1,0:T(4,128)(2,1)S(1)}, u32[]{:S(2)}, u32[]{:S(2)}) async-start(bf16[16,4,8192]{2,1,0:T(4,128)(2,1)} %all_to_all.42), calls=%async_computation | async-start | bytes 2097152 | tf_op jit(solution)/shard_map/all_to_all | solution.py:326
  21.0 6.0 %all-gather = bf16[1,8192]{1,0:T(2,128)(2,1)S(1)} all-gather(bf16[1,2048]{1,0:T(2,128)(2,1)S(1)} %copy-done.12), channel_id=2, replica_groups=mesh['section'=2,'dp'=4,'tensor'=16] {'dp'}, dimensions={1}, use_global_device_ids=true | all-gather | bytes 20480 | tf_op jit(solution)/shard_map/all_gather | solution.py:313
  27.0 5.9 %all-gather.1 = bf16[1,8192,16]{1,2,0:T(8,128)(2,1)S(1)} all-gather(bf16[1,2048,16]{1,2,0:T(8,128)(2,1)S(1)} %copy-done.11), channel_id=3, replica_groups=mesh['section'=2,'dp'=4,'tensor'=16] {'dp'}, dimensions={1}, use_global_device_ids=true | all-gather | bytes 327680 | tf_op jit(solution)/shard_map/all_gather | solution.py:312
  32.9 1.8 bitcast_convert_fusion
  35.3 0.6 mul.369
  36.0 0.6 mul.387
  36.9 2.5 fusion.40
  39.7 2.3 all_to_all.48
  42.0 1.2 all_to_all.45
  43.4 6.9 %all-to-all-start.2 = ((bf16[16,4,8192]{2,1,0:T(4,128)(2,1)}), bf16[16,4,8192]{2,1,0:T(4,128)(2,1)S(1)}, u32[]{:S(2)}, u32[]{:S(2)}) async-start(bf16[16,4,8192]{2,1,0:T(4,128)(2,1)} %all_to_all.48), calls=%async_computation.2 | async-start | bytes 2097152 | tf_op jit(solution)/shard_map/all_to_all | solution.py:326
  51.3 15.8 %all-to-all-done.2 = bf16[16,4,8192]{2,1,0:T(4,128)(2,1)S(1)} async-done(((bf16[16,4,8192]{2,1,0:T(4,128)(2,1)}), bf16[16,4,8192]{2,1,0:T(4,128)(2,1)S(1)}, u32[]{:S(2)}, u32[]{:S(2)}) %all-to-all-start.2) | async-done | bytes 1048608 | tf_op jit(solution)/shard_map/all_to_all | solution.py:326
  67.0 4.4 %all-to-all-start.1 = ((bf16[16,4,8192]{2,1,0:T(4,128)(2,1)}), bf16[16,4,8192]{2,1,0:T(4,128)(2,1)}, u32[]{:S(2)}, u32[]{:S(2)}) async-start(bf16[16,4,8192]{2,1,0:T(4,128)(2,1)} %all_to_all.45), calls=%async_computation.1 | async-start | bytes 2097152 | tf_op jit(solution)/shard_map/all_to_all | solution.py:326
  71.7 2.6 mul.400
  74.2 3.0 mul.401
  77.2 3.1 scatter_custom_fusion
  80.4 2.3 all_to_all.51
  83.9 1.1 fusion.57
  85.2 1.7 gather_fusion
  86.9 1.7 reshape.230
  88.6 1.2 reduce_sum.255
  90.4 6.7 %all-to-all-start.3 = ((bf16[16,4,8192]{2,1,0:T(4,128)(2,1)}), bf16[16,4,8192]{2,1,0:T(4,128)(2,1)}, u32[]{:S(2)}, u32[]{:S(2)}) async-start(bf16[16,4,8192]{2,1,0:T(4,128)(2,1)} %all_to_all.51), calls=%async_computation.3 | async-start | bytes 2097152 | tf_op jit(solution)/shard_map/all_to_all | solution.py:373
  97.1 1.2 fusion.10
  98.2 1.5 collective-permute-start
  100.4 1.7 gather_fusion.2
  102.1 1.7 reshape.234
  103.8 2.1 reduce_sum.271
  105.9 1.3 all_to_all.47
  107.3 0.9 gather_fusion.1
  108.2 0.7 reshape.232
  108.8 2.1 reduce_sum.263
  111.0 1.1 all-to-all-done.3
  112.1 2.1 stack.28
  114.2 1.1 bitcast_select_fusion.1
  115.3 2.5 fusion.41
  118.8 0.7 mul.408
  119.5 1.7 scatter_custom_fusion.1
  121.2 1.2 all_to_all.53
  122.4 5.6 %all-to-all-start.4 = ((bf16[16,4,8192]{2,1,0:T(4,128)(2,1)}), bf16[16,4,8192]{2,1,0:T(4,128)(2,1)S(1)}, u32[]{:S(2)}, u32[]{:S(2)}) async-start(bf16[16,4,8192]{2,1,0:T(4,128)(2,1)} %all_to_all.53), calls=%async_computation.4 | async-start | bytes 2097152 | tf_op jit(solution)/shard_map/all_to_all | solution.py:373
  129.0 0.9 fusion.20
  129.9 1.5 collective-permute-start.1
  131.8 7.7 %collective-permute-done.1 = bf16[16,8192]{1,0:T(8,128)(2,1)} collective-permute-done((bf16[16,8192]{1,0:T(8,128)(2,1)}, bf16[16,8192]{1,0:T(8,128)(2,1)}, u32[]{:S(2)}, u32[]{:S(2)}) %collective-permute-start.1) | collective-permute-done | bytes 262176 | tf_op jit(solution)/shard_map/ppermute | solution.py:287
  139.4 1.1 bitcast_select_fusion
  140.5 2.6 fusion.42
  143.4 1.0 fusion
  144.4 1.0 fusion.33
  145.5 0.7 broadcast_multiply_fusion.3
  146.9 1.7 mul.415
  148.6 2.4 scatter_custom_fusion.2
  151.0 1.2 all_to_all.55
  152.2 2.2 pad_maximum_fusion
  154.5 6.5 %all-to-all-start.5 = ((bf16[16,4,8192]{2,1,0:T(4,128)(2,1)}), bf16[16,4,8192]{2,1,0:T(4,128)(2,1)S(1)}, u32[]{:S(2)}, u32[]{:S(2)}) async-start(bf16[16,4,8192]{2,1,0:T(4,128)(2,1)} %all_to_all.55), calls=%async_computation.5 | async-start | bytes 2097152 | tf_op jit(solution)/shard_map/all_to_all | solution.py:373
  161.0 113.1 %shard_map.153 = (bf16[3,256,512]{2,1,0:T(8,128)(2,1)}, bf16[3,256,512]{2,1,0:T(8,128)(2,1)}, f32[512,2048]{1,0:T(8,128)}) custom-call(bf16[3,16,8192]{2,1,0:T(8,128)(2,1)} %get-tuple-element.32.passed_ref, bf16[3,256,512]{2,1,0:T(8,128)(2,1)} %bitcast.177, bf16[3,256,512]{2,1,0:T(8,128)(2,1)} %bitcast.178, bf16[512,8192]{1,0:T(8,128)(2,1)} %bitcast.176), custom_call_target="tpu_custom_call" | custom-call | flops 12999999488 | bytes 30000000 | tf_op jit(solution)/shard_map/pallas_call | solution.py:246
  274.2 9.9 %all-reduce = bf16[8192]{0:T(1024)(128)(2,1)S(1)} all-reduce(bf16[8192]{0:T(1024)(128)(2,1)S(1)} %add_convert_fusion), channel_id=5, replica_groups=mesh['section'=2,'dp'=4,'tensor'=16] {'dp'}, use_global_device_ids=true, to_apply=%region_36.37.clone | all-reduce | flops 8192 | bytes 32768
  284.0 31.5 %psum.17 = bf16[2048]{0:T(1024)(128)(2,1)S(1)} all-reduce(bf16[2048]{0:T(1024)(128)(2,1)S(1)} %dynamic-slice.1), channel_id=1, replica_groups=mesh['section'=2,'dp'=4,'tensor'=16] {'tensor'}, use_global_device_ids=true, to_apply=%region_35.36 | all-reduce | flops 2048 | bytes 8192 | tf_op jit(solution)/shard_map/psum | solution.py:380
  315.6 0.6 broadcast_in_dim.30
  316.2 34.5 %all-reduce.3.cloned.1.call-done = bf16[2048,16]{0,1:T(8,128)(2,1)} async-done(((bf16[2048,16]{0,1:T(8,128)(2,1)}), bf16[2048,16]{0,1:T(8,128)(2,1)}) %all-reduce.3.cloned.1.call-update) | async-done | bytes 65552 | tf_op jit(solution)/shard_map/psum | solution.py:379
  350.7 1.5 bitcast_convert_fusion.1
  352.2 1.1 stack.29
  353.6 3.7 %maximum_bitcast_fusion = bf16[1,3,64,8192]{3,2,1,0:T(8,128)(2,1)} fusion(bf16[1,64,8192]{2,1,0:T(8,128)(2,1)S(1)} %stack.30, bf16[1,64,8192]{2,1,0:T(8,128)(2,1)} %stack.29, bf16[1,64,8192]{2,1,0:T(8,128)(2,1)} %stack.28), kind=kLoop, calls=%fused_computation.12 | loop fusion | flops 3145728 | bytes 6291456 | tf_op jit(solution)/shard_map/broadcast_in_dim | solution.py:394
  357.3 0.9 copy.87
  358.2 0.9 copy.88
  359.1 2.0 copy.89
  (121 shorter events, 9.2 us)
Async XLA Ops:
  10.3 9.8 %copy-start = (bf16[1,3,16,8192]{3,2,1,0:T(8,128)(2,1)S(1)}, bf16[1,3,16,8192]{3,2,1,0:T(8,128)(2,1)}, u32[]{:S(2)}) copy-start(bf16[1,3,16,8192]{3,2,1,0:T(8,128)(2,1)} %param.11) | copy-start | bytes 2359300
  10.3 10.0 %copy-start.13 = (s32[1,3,16,2]{2,3,1,0:T(2,128)S(1)}, s32[1,3,16,2]{2,3,1,0:T(2,128)}, u32[]{:S(2)}) copy-start(s32[1,3,16,2]{2,3,1,0:T(2,128)} %param.13) | copy-start | bytes 1156
  10.3 10.7 %copy-start.12 = (bf16[1,2048]{1,0:T(2,128)(2,1)S(1)}, bf16[1,2048]{1,0:T(2,128)(2,1)}, u32[]{:S(2)}) copy-start(bf16[1,2048]{1,0:T(2,128)(2,1)} %param.19) | copy-start | bytes 12292
  10.3 16.7 %copy-start.11 = (bf16[1,2048,16]{1,2,0:T(8,128)(2,1)S(1)}, bf16[1,2048,16]{1,2,0:T(8,128)(2,1)}, u32[]{:S(2)}) copy-start(bf16[1,2048,16]{1,2,0:T(8,128)(2,1)} %param.18) | copy-start | bytes 196612
  11.5 31.9 %all-to-all-start = ((bf16[16,4,8192]{2,1,0:T(4,128)(2,1)}), bf16[16,4,8192]{2,1,0:T(4,128)(2,1)S(1)}, u32[]{:S(2)}, u32[]{:S(2)}) async-start(bf16[16,4,8192]{2,1,0:T(4,128)(2,1)} %all_to_all.42), calls=%async_computation | async-start | bytes 2097152 | tf_op jit(solution)/shard_map/all_to_all | solution.py:326
  39.3 4.0 %copy-start.16 = (s32[32,1]{0,1:T(1,128)S(1)}, s32[32,1]{0,1:T(1,128)}, u32[]{:S(2)}) copy-start(s32[32,1]{0,1:T(1,128)} %mul.369) | copy-start | bytes 388
  39.7 10.8 %copy-start.15 = (s32[32,1]{0,1:T(1,128)S(1)}, s32[32,1]{0,1:T(1,128)}, u32[]{:S(2)}) copy-start(s32[32,1]{0,1:T(1,128)} %mul.387) | copy-start | bytes 388
  43.4 23.7 %all-to-all-start.2 = ((bf16[16,4,8192]{2,1,0:T(4,128)(2,1)}), bf16[16,4,8192]{2,1,0:T(4,128)(2,1)S(1)}, u32[]{:S(2)}, u32[]{:S(2)}) async-start(bf16[16,4,8192]{2,1,0:T(4,128)(2,1)} %all_to_all.48), calls=%async_computation.2 | async-start | bytes 2097152 | tf_op jit(solution)/shard_map/all_to_all | solution.py:326
  50.5 0.5 copy-start.14
  67.0 13.3 %copy-start.2 = (bf16[16,4,8192]{2,1,0:T(4,128)(2,1)}, bf16[16,4,8192]{2,1,0:T(4,128)(2,1)S(1)}, u32[]{:S(2)}) copy-start(bf16[16,4,8192]{2,1,0:T(4,128)(2,1)S(1)} %all-to-all-done.2) | copy-start | bytes 3145732
  67.0 23.3 %all-to-all-start.1 = ((bf16[16,4,8192]{2,1,0:T(4,128)(2,1)}), bf16[16,4,8192]{2,1,0:T(4,128)(2,1)}, u32[]{:S(2)}, u32[]{:S(2)}) async-start(bf16[16,4,8192]{2,1,0:T(4,128)(2,1)} %all_to_all.45), calls=%async_computation.1 | async-start | bytes 2097152 | tf_op jit(solution)/shard_map/all_to_all | solution.py:326
  74.2 8.4 %copy-start.17 = (u32[128]{0:T(128)S(1)}, u32[128]{0:T(128)}, u32[]{:S(2)}) copy-start(u32[128]{0:T(128)} %constant.56) | copy-start | bytes 1540
  89.8 10.3 %copy-start.3 = (bf16[16,4,8192]{2,1,0:T(4,128)(2,1)S(1)}, bf16[16,4,8192]{2,1,0:T(4,128)(2,1)}, u32[]{:S(2)}) copy-start(bf16[16,4,8192]{2,1,0:T(4,128)(2,1)} %copy-done.2) | copy-start | bytes 3145732
  90.4 21.7 %all-to-all-start.3 = ((bf16[16,4,8192]{2,1,0:T(4,128)(2,1)}), bf16[16,4,8192]{2,1,0:T(4,128)(2,1)}, u32[]{:S(2)}, u32[]{:S(2)}) async-start(bf16[16,4,8192]{2,1,0:T(4,128)(2,1)} %all_to_all.51), calls=%async_computation.3 | async-start | bytes 2097152 | tf_op jit(solution)/shard_map/all_to_all | solution.py:373
  98.2 3.9 %copy-start.7 = (bf16[16,8192]{1,0:T(8,128)(2,1)}, bf16[16,8192]{1,0:T(8,128)(2,1)S(1)}, u32[]{:S(2)}) copy-start(bf16[16,8192]{1,0:T(8,128)(2,1)S(1)} %fusion.10) | copy-start | bytes 786436
  98.2 16.0 %collective-permute-start = (bf16[16,8192]{1,0:T(8,128)(2,1)S(1)}, bf16[16,8192]{1,0:T(8,128)(2,1)}, u32[]{:S(2)}, u32[]{:S(2)}) collective-permute-start(bf16[16,8192]{1,0:T(8,128)(2,1)S(1)} %fusion.10), channel_id=1, source_target_pairs={{64,0},{65,1},{66,2},{67,3},{68,4},{69,5},{70,6},{71,7},{72,8},{73... | collective-permute-start | bytes 786440 | tf_op jit(solution)/shard_map/ppermute | solution.py:287
  121.2 6.9 %copy-start.5 = (f32[16,8192]{1,0:T(8,128)S(1)}, f32[16,8192]{1,0:T(8,128)}, u32[]{:S(2)}) copy-start(f32[16,8192]{1,0:T(8,128)} %reduce_sum.263) | copy-start | bytes 1572868
  122.4 9.0 %copy-start.4 = (f32[8192,16]{0,1:T(8,128)S(1)}, f32[8192,16]{0,1:T(8,128)}, u32[]{:S(2)}) copy-start(f32[8192,16]{0,1:T(8,128)} %fusion.57) | copy-start | bytes 1572868
  122.4 32.0 %all-to-all-start.4 = ((bf16[16,4,8192]{2,1,0:T(4,128)(2,1)}), bf16[16,4,8192]{2,1,0:T(4,128)(2,1)S(1)}, u32[]{:S(2)}, u32[]{:S(2)}) async-start(bf16[16,4,8192]{2,1,0:T(4,128)(2,1)} %all_to_all.53), calls=%async_computation.4 | async-start | bytes 2097152 | tf_op jit(solution)/shard_map/all_to_all | solution.py:373
  128.0 146.1 %reduce-scatter.2.cloned.1.call-start = ((), (), s32[]{:S(2)}) async-start(), calls=%async_computation.7 | async-start | bytes 327680 | tf_op jit(solution)/shard_map/reduce_scatter | solution.py:383
  129.9 9.6 %collective-permute-start.1 = (bf16[16,8192]{1,0:T(8,128)(2,1)}, bf16[16,8192]{1,0:T(8,128)(2,1)}, u32[]{:S(2)}, u32[]{:S(2)}) collective-permute-start(bf16[16,8192]{1,0:T(8,128)(2,1)} %fusion.20), channel_id=1, source_target_pairs={{64,0},{65,1},{66,2},{67,3},{68,4},{69,5},{70,6},{71,7},{72,8},{73... | collective-permute-start | bytes 786440 | tf_op jit(solution)/shard_map/ppermute | solution.py:287
  140.5 3.9 %copy-start.6 = (f32[16,8192]{1,0:T(8,128)S(1)}, f32[16,8192]{1,0:T(8,128)}, u32[]{:S(2)}) copy-start(f32[16,8192]{1,0:T(8,128)} %reduce_sum.271) | copy-start | bytes 1572868
  146.9 5.3 %copy-start.8 = (bf16[16,8192]{1,0:T(8,128)(2,1)S(1)}, bf16[16,8192]{1,0:T(8,128)(2,1)}, u32[]{:S(2)}) copy-start(bf16[16,8192]{1,0:T(8,128)(2,1)} %copy-done.7) | copy-start | bytes 786436
  154.5 198.9 %all-to-all-start.5 = ((bf16[16,4,8192]{2,1,0:T(4,128)(2,1)}), bf16[16,4,8192]{2,1,0:T(4,128)(2,1)S(1)}, u32[]{:S(2)}, u32[]{:S(2)}) async-start(bf16[16,4,8192]{2,1,0:T(4,128)(2,1)} %all_to_all.55), calls=%async_computation.5 | async-start | bytes 2097152 | tf_op jit(solution)/shard_map/all_to_all | solution.py:373
  161.0 189.8 %all-reduce.3.cloned.1.call-start = ((), (), s32[]{:S(2)}) async-start(), calls=%async_computation.8 | async-start | bytes 131072 | tf_op jit(solution)/shard_map/psum | solution.py:379
  353.6 3.7 %copy-start.10 = (bf16[3,256,512]{2,1,0:T(8,128)(2,1)S(1)}, bf16[3,256,512]{2,1,0:T(8,128)(2,1)}, u32[]{:S(2)}) copy-start(bf16[3,256,512]{2,1,0:T(8,128)(2,1)} %get-tuple-element.10) | copy-start | bytes 2359300
  353.6 4.6 %copy-start.9 = (bf16[3,256,512]{2,1,0:T(8,128)(2,1)S(1)}, bf16[3,256,512]{2,1,0:T(8,128)(2,1)}, u32[]{:S(2)}) copy-start(bf16[3,256,512]{2,1,0:T(8,128)(2,1)} %get-tuple-element.11) | copy-start | bytes 2359300
  353.6 5.5 %copy-start.1 = (f32[512,2048]{1,0:T(8,128)S(1)}, f32[512,2048]{1,0:T(8,128)}, u32[]{:S(2)}) copy-start(f32[512,2048]{1,0:T(8,128)} %get-tuple-element.12) | copy-start | bytes 12582916
Sparse Core Ops, SparseCore 0:
  145.6 20.8 reduce-scatter.1
  274.3 76.4 all-reduce.2
where the time goes:
time: 370 us; the launch traced here: 368 us
  Pallas kernels  113 us (31%)
  waiting for transfers between devices  59.2 us (16%)
  blocking collectives  53.2 us (14%)
  local copies, waits for them, and re-layouts  43.1 us (12%)
  starting transfers between devices  41.8 us (11%)
  other arithmetic  29.4 us (8%)
  between operations  15.3 us (4%)
  matrix products  12.8 us (3%)
    pallas_call x1, Pallas kernels, mixer(): pl.pallas_call(mixer_kernel, out_shape=(jax.ShapeDtypeStruct((3, 256, 512...  113 us
    psum x1, waiting for transfers between devices, on_device(): lax.psum(router_acc.astype(jnp.bfloat16), 'tensor').astype(jnp.float32)  34.5 us
    psum x1, blocking collectives, on_device(): lax.psum(gain_acc.astype(jnp.bfloat16), 'tensor').astype(jnp.float32)  31.5 us
    all_to_all x3, starting transfers between devices, on_device(): lax.all_to_all(expert_back[0, micro_step], 'tensor', split_axis=0, concat...  20 us
    all_to_all x3, starting transfers between devices, on_device(): lax.all_to_all(send_buffer, 'tensor', split_axis=0, concat_axis=0, tiled=...  18.8 us
    all_to_all x3, waiting for transfers between devices, on_device(): lax.all_to_all(expert_back[0, micro_step], 'tensor', split_axis=0, concat...  15.8 us
    unnamed x1, blocking collectives  9.86 us
    mul x9, local copies, waits for them, and re-layouts, on_device(): route_prob[:, :, None] * upstream_f[:, None, :]  9.05 us
  transfers between devices with their start and end apart: 10, of which 4 were waited for; matrix products, arithmetic and copies ran while one was open for 15% of the time, Pallas kernels for 31%

commit v1 on v0

v1 whole, which is shorter than its diff:
```python
import jax
import jax.numpy as jnp
from jax import lax
from jax.experimental import pallas as pl
from jax.experimental.pallas import tpu as pltpu
from jax.sharding import PartitionSpec as P

MESH = pl.DeviceIdType.MESH
MICRO = 3
TOK = 16
WIDTH = 8192
EXPERTS = 16
SLOTS = 64
QB = 2048
CHUNKS = 8
QCOL = 256
CCOL = 1024
HALF = 512
OUTV = 4
WBUF = 3
F32 = jnp.float32
BF16 = jnp.bfloat16


def dot(a, b, dims):
    return lax.dot_general(a, b, ((dims[0], dims[1]), ((), ())), preferred_element_type=F32)


def iota(shape, dim):
    return lax.broadcasted_iota(jnp.int32, shape, dim)


def layer_kernel(
    inc_hbm, hid_ref, eo_ref, routes_ref, routes_t_ref, back_hbm, scan_ref, gate_ref, w_hbm, rg_ref,
    passed_out, scan_out, gate_out, exp_out, wgrad_out, rg_out,
    G, W, gT, inner, own, outv, msend, mrecv, xsend, xrecv, stage,
    UP, PO, NR, RG, NG, RGA, RA, RB, RBR, RC, BR1, BR2, BP, DS, DR, DP,
    probs_s, prob64_s, sel_s, selb_s, inv_s,
    ag_s, ag_r, w_sem, ms_s, ms_r, xs_s, xs_r, out_sem, fin_sem, po_sem,
    b1_s, b1_r, b2_s, b2_r, d1_s, d1_r, d2_s, d2_r, rg_s, rg_r, up_l, up_s, up_r,
    ra_s, ra_r, rb_s, rb_r, rc_s, rc_r,
):
    sec = lax.axis_index("section")
    d = lax.axis_index("dp")
    tau = lax.axis_index("tensor")
    z = tau // 4
    y = tau % 4
    core = d % 2
    xl = d // 2
    mate = xl * 2 + (1 - core)
    xnbr = (1 - xl) * 2 + core

    def at_y(k):
        return z * 4 + (y + k) % 4

    def at_z(k):
        return ((z + k) % 4) * 4 + y

    def al(v, m):
        return pl.multiple_of(v, m)

    def rows16(v):
        return pl.ds(al(16 * v, 16), 16)

    def remote(src, dst, ssem, rsem, peer):
        return pltpu.make_async_remote_copy(
            src_ref=src, dst_ref=dst, send_sem=ssem, recv_sem=rsem, device_id=peer, device_id_type=MESH
        )

    barrier = pltpu.get_barrier_semaphore()

    def greet(k, carry):
        pl.semaphore_signal(barrier, inc=1, device_id={"tensor": (tau + k) % 16}, device_id_type=MESH)
        return carry

    lax.fori_loop(1, 16, greet, 0)
    for k in range(1, 4):
        pl.semaphore_signal(barrier, inc=1, device_id={"dp": (d + k) % 4}, device_id_type=MESH)
    pl.semaphore_signal(barrier, inc=1, device_id={"section": 1 - sec}, device_id_type=MESH)

    def up_local(t):
        return pltpu.make_async_copy(inc_hbm.at[t], UP.at[t], up_l.at[t])

    up_local(0).start()

    @pl.when(sec == 1)
    def _():
        up_local(1).start()
        up_local(2).start()

    def w_start(c):
        for q in range(4):
            pltpu.make_async_copy(
                w_hbm.at[:, pl.ds(al(q * QB + c * QCOL, QCOL), QCOL)],
                W.at[c % WBUF, :, pl.ds(q * QCOL, QCOL)],
                w_sem.at[c % WBUF],
            ).start()

    def b1_copy(t, k, recv):
        if recv:
            ref = BR1.at[t, rows16((z + 4 - k) % 4)]
            return remote(ref, ref, b1_s.at[t, k], b1_r.at[t, k], {"tensor": at_z(k)})
        return remote(
            back_hbm.at[t, rows16((z + k) % 4)], BR1.at[t, rows16(z)],
            b1_s.at[t, k], b1_r.at[t, k], {"tensor": at_z(k)},
        )

    def b1_local(t):
        return pltpu.make_async_copy(back_hbm.at[t, rows16(z)], BR1.at[t, rows16(z)], b1_r.at[t, 0])

    def b2_copy(t, k, recv):
        if recv:
            ref = BR2.at[t, rows16((y + 4 - k) % 4)]
            return remote(ref, ref, b2_s.at[t, k], b2_r.at[t, k], {"tensor": at_y(k)})
        return remote(
            BP.at[t % 2, rows16((y + k) % 4)], BR2.at[t, rows16(y)],
            b2_s.at[t, k], b2_r.at[t, k], {"tensor": at_y(k)},
        )

    def d1_copy(t, k, recv):
        if recv:
            ref = DR.at[t, rows16((y + 4 - k) % 4)]
            return remote(ref, ref, d1_s.at[t, k], d1_r.at[t, k], {"tensor": at_y(k)})
        return remote(
            DS.at[t % 2, rows16((y + k) % 4)], DR.at[t, rows16(y)],
            d1_s.at[t, k], d1_r.at[t, k], {"tensor": at_y(k)},
        )

    def d2_copy(t, k, recv):
        if recv:
            ref = exp_out.at[t, rows16((z + 4 - k) % 4)]
            return remote(ref, ref, d2_s.at[t, k], d2_r.at[t, k], {"tensor": at_z(k)})
        return remote(
            DP.at[t % 2, rows16((z + k) % 4)], exp_out.at[t, rows16(z)],
            d2_s.at[t, k], d2_r.at[t, k], {"tensor": at_z(k)},
        )

    def d2_local(t):
        return pltpu.make_async_copy(DP.at[t % 2, rows16(z)], exp_out.at[t, rows16(z)], d2_r.at[t, 0])

    def rg_copy(k, recv):
        ref = RG.at[(d + 4 - k) % 4] if recv else RG.at[d]
        return remote(ref if recv else rg_ref, ref, rg_s.at[k], rg_r.at[k], {"dp": (d + k) % 4})

    pl.semaphore_wait(barrier, 19)

    for k in range(1, 4):
        rg_copy(k, False).start()
    for t in range(MICRO):
        for k in (2, 1, 3):
            b1_copy(t, k, False).start()
        b1_local(t).start()
    for c in range(WBUF):
        w_start(c)
    RG[d] = rg_ref[...]

    slot_r = iota((SLOTS, TOK), 0)
    slot_e = ((slot_r >> 2) & 3) * 4 + (slot_r >> 4)
    slot_c = slot_r & 3
    slot_rb = iota((TOK, SLOTS), 1)
    slot_eb = ((slot_rb >> 2) & 3) * 4 + (slot_rb >> 4)
    slot_cb = slot_rb & 3
    perm_in = iota((SLOTS, SLOTS), 1)
    perm_out = iota((SLOTS, SLOTS), 0)
    perm = (perm_in == ((perm_out >> 2) & 3) * 16 + (perm_out >> 4) * 4 + (perm_out & 3)).astype(F32).astype(BF16)
    upper = (iota((TOK, TOK), 0) < iota((TOK, TOK), 1)).astype(F32).astype(BF16)
    lower = (iota((TOK, TOK), 0) > iota((TOK, TOK), 1)).astype(F32).astype(BF16)

    RGA[...] = jnp.zeros_like(RGA)
    for k in range(1, 4):
        rg_copy(k, True).wait_recv()

    def gain_of(q):
        return RG[q, EXPERTS : EXPERTS + 1, :].astype(F32)

    def hid_of(t, q):
        return hid_ref[t, :, q * QB : (q + 1) * QB].astype(F32)

    def prepare(t, carry):
        total = jnp.zeros((TOK, 1), F32)
        for q in range(4):
            h = hid_of(t, q)
            total += jnp.sum(h * h, axis=1, keepdims=True)
        inv = 1.0 / jnp.sqrt(total / WIDTH + 1e-05)
        inv_s[t] = inv
        logits = jnp.zeros((TOK, EXPERTS), F32)
        logits_t = jnp.zeros((EXPERTS, TOK), F32)
        for q in range(4):
            normed = (hid_of(t, q) * inv * gain_of(q)).astype(BF16)
            NR[t, :, q * QB : (q + 1) * QB] = normed
            router = RG[q, 0:EXPERTS, :]
            logits += dot(normed, router, ((1,), (1,)))
            logits_t += dot(router, normed, ((1,), (1,)))
        weights = jnp.exp(logits)
        probs_s[t] = weights / jnp.sum(weights, axis=1, keepdims=True)
        weights_t = jnp.exp(logits_t)
        probs_t = weights_t / jnp.sum(weights_t, axis=0, keepdims=True)
        spread = jnp.zeros((SLOTS, TOK), F32)
        for e in range(EXPERTS):
            spread = jnp.where(slot_e == e, probs_t[e : e + 1, :], spread)
        rt0 = routes_t_ref[t, 0:1, :]
        rt1 = routes_t_ref[t, 1:2, :]
        named = ((rt0 == slot_e) | (rt1 == slot_e)).astype(F32)
        before = dot(named.astype(BF16), upper, ((1,), (0,)))
        sel = jnp.where(before == slot_c.astype(F32), named, 0.0)
        sel_s[t] = sel.astype(BF16)
        prob64_s[t] = jnp.sum(sel * spread, axis=1, keepdims=True)
        r0 = routes_ref[t, :, 0:1]
        r1 = routes_ref[t, :, 1:2]
        named_b = ((r0 == slot_eb) | (r1 == slot_eb)).astype(F32)
        before_b = dot(lower, named_b.astype(BF16), ((1,), (0,)))
        selb_s[t] = jnp.where(before_b == slot_cb.astype(F32), named_b, 0.0).astype(BF16)
        return carry

    lax.fori_loop(0, MICRO, prepare, 0)

    def dispatch(t):
        @pl.when(t >= 2)
        def _():
            for k in range(1, 4):
                d1_copy(t - 2, k, False).wait_send()

        prob = prob64_s[t]
        sel = sel_s[t]
        for q in range(4):
            cols = slice(q * QB, (q + 1) * QB)
            DS[t % 2, :, cols] = (dot(sel, UP[t, :, cols], ((1,), (0,))) * prob).astype(BF16)
        for k in (2, 1, 3):
            d1_copy(t, k, False).start()
        DR[t, rows16(y), :] = DS[t % 2, rows16(y), :]

    def dispatch_relay(t):
        for k in range(1, 4):
            d1_copy(t, k, True).wait_recv()

        @pl.when(t >= 2)
        def _():
            for k in range(1, 4):
                d2_copy(t - 2, k, False).wait_send()
            d2_local(t - 2).wait()

        for q in range(4):
            cols = slice(q * QB, (q + 1) * QB)
            DP[t % 2, :, cols] = dot(perm, DR[t, :, cols], ((1,), (0,))).astype(BF16)
        for k in (2, 1, 3):
            d2_copy(t, k, False).start()
        d2_local(t).start()

    def back_relay(t):
        for k in range(1, 4):
            b1_copy(t, k, True).wait_recv()
        b1_local(t).wait()

        @pl.when(t >= 2)
        def _():
            for k in range(1, 4):
                b2_copy(t - 2, k, False).wait_send()

        for q in range(4):
            cols = slice(q * QB, (q + 1) * QB)
            BP[t % 2, :, cols] = dot(perm, BR1[t, :, cols], ((1,), (0,))).astype(BF16)
        for k in (2, 1, 3):
            b2_copy(t, k, False).start()
        BR2[t, rows16(y), :] = BP[t % 2, rows16(y), :]

    def up_copy(t):
        return remote(PO.at[t - 1], UP.at[t], up_s.at[t], up_r.at[t], {"section": 1 - sec})

    def po_copy(t):
        return pltpu.make_async_copy(PO.at[t], passed_out.at[t], po_sem.at[t])

    def upstream_ready(t):
        @pl.when((sec == 1) | (t == 0))
        def _():
            up_local(t).wait()

        @pl.when((sec == 0) & (t > 0))
        def _():
            up_copy(t).wait_recv()

    def combine(t):
        for k in range(1, 4):
            b2_copy(t, k, True).wait_recv()
        scores = jnp.zeros((TOK, 2 * TOK), F32)
        for q in range(4):
            cols = slice(q * QB, (q + 1) * QB)
            scores += dot(UP[t, :, cols], eo_ref[t, :, cols], ((1,), (1,)))
        row_i = iota((TOK, 2 * TOK), 0)
        col_i = iota((TOK, 2 * TOK), 1)
        s0 = jnp.sum(jnp.where(col_i == 2 * row_i, scores, 0.0), axis=1, keepdims=True)
        s1 = jnp.sum(jnp.where(col_i == 2 * row_i + 1, scores, 0.0), axis=1, keepdims=True)
        expert_i = iota((TOK, EXPERTS), 1)
        prob_grad = jnp.where(routes_ref[t, :, 0:1] == expert_i, s0, 0.0) + jnp.where(
            routes_ref[t, :, 1:2] == expert_i, s1, 0.0
        )
        probs = probs_s[t]
        logit_grad = (
            probs * (prob_grad - jnp.sum(probs * prob_grad, axis=1, keepdims=True))
        ).astype(BF16)
        inv = inv_s[t]
        selb = selb_s[t]
        mean = jnp.zeros((TOK, 1), F32)
        for q in range(4):
            cols = slice(q * QB, (q + 1) * QB)
            norm_grad = dot(logit_grad, RG[q, 0:EXPERTS, :], ((1,), (0,))) + dot(
                selb, BR2[t, :, cols], ((1,), (0,))
            )
            NG[:, cols] = norm_grad
            h = hid_of(t, q)
            mean += jnp.sum(norm_grad * gain_of(q) * h, axis=1, keepdims=True)
            RGA[q, EXPERTS : EXPERTS + 1, :] += jnp.sum(norm_grad * h * inv, axis=0, keepdims=True)
            RGA[q, 0:EXPERTS, :] += dot(logit_grad, NR[t, :, cols], ((0,), (0,)))
        mean = mean / WIDTH
        for q in range(4):
            cols = slice(q * QB, (q + 1) * QB)
            hidden_grad = inv * (NG[:, cols] * gain_of(q)) - hid_of(t, q) * (inv * inv * inv) * mean
            passed = (UP[t, :, cols].astype(F32) + hidden_grad).astype(BF16)
            PO[t, :, cols] = passed
            for c in range(CHUNKS):
                G[c, t, z, rows16(y), q * QCOL : (q + 1) * QCOL] = passed[:, c * QCOL : (c + 1) * QCOL]

        @pl.when((sec == 1) & (t < MICRO - 1))
        def _():
            up_copy(t + 1).start()

        po_copy(t).start()

    upstream_ready(0)

    def front(s, carry):
        @pl.when(s == 0)
        def _():
            dispatch(0)

        @pl.when(s < MICRO)
        def _():
            back_relay(s)

        @pl.when(s >= 1)
        def _():
            @pl.when(s >= 2)
            def _():
                upstream_ready(s - 1)

            combine(s - 1)

        @pl.when(s >= 2)
        def _():
            dispatch(s - 1)

        @pl.when((s == 1) | (s == 3))
        def _():
            dispatch_relay((s - 1) // 2)

        return carry

    for t in range(MICRO):
        gate_f = gate_ref[t].astype(F32)
        gated = scan_ref[t].astype(F32) * gate_f * jax.nn.sigmoid(gate_f)
        gT[:, t * 256 : (t + 1) * 256] = gated.T.astype(BF16)
    inner[...] = jnp.zeros_like(inner)
    lax.fori_loop(0, MICRO + 1, front, 0)

    def shard(c, h, k, c0, cw):
        cols = pl.ds(h * HALF + c0, cw)
        if h == 0:
            return G.at[c, :, z, rows16((y + k) % 4), cols]
        return G.at[c, :, (z + k) % 4, rows16(y), cols]

    def block(c, h, k, c0, cw):
        cols = pl.ds(h * HALF + c0, cw)
        if h == 0:
            return G.at[c, :, (z + k) % 4, :, cols]
        return G.at[c, :, :, rows16((y + k) % 4), cols]

    def ag_copy(c, h, kind, k):
        fn = shard if kind < 4 else block
        if kind % 4 < 2:
            ref = fn(c, h, k, 0, HALF)
        else:
            ref = fn(c, h, k, (kind % 2) * (HALF // 2), HALF // 2)
        step = 1 if kind % 2 == 0 else 3
        peer = at_y(step) if (h == 0) == (kind < 4) else at_z(step)
        return remote(ref, ref, ag_s.at[c, h, kind], ag_r.at[c, h, kind], {"tensor": peer})

    def send_step(kind):
        return 0 if kind % 4 < 2 else (3 if kind % 2 == 0 else 1)

    def send(c, h, kind):
        ag_copy(c, h, kind, send_step(kind)).start()

    def recv(c, h, kind):
        step = (3 if kind % 2 == 0 else 1) if kind % 4 < 2 else 2
        ag_copy(c, h, kind, step).wait_recv()

    def t0(c):
        for h in range(2):
            send(c, h, 0)
            send(c, h, 1)

    def t1(c):
        for h in range(2):
            recv(c, h, 0)
            send(c, h, 2)
            recv(c, h, 1)
            send(c, h, 3)

    def t2(c):
        for h in range(2):
            recv(c, h, 2)
            recv(c, h, 3)
            send(c, h, 4)
            send(c, h, 5)

    def t3(c):
        for h in range(2):
            recv(c, h, 4)
            send(c, h, 6)
            recv(c, h, 5)
            send(c, h, 7)

    def mate_copy(c):
        return remote(msend.at[c % 2], mrecv.at[c], ms_s.at[c], ms_r.at[c], {"dp": mate})

    def x_copy(c):
        return remote(xsend.at[c % 2], xrecv.at[c], xs_s.at[c], xs_r.at[c], {"dp": xnbr})

    def out_copy(c):
        return pltpu.make_async_copy(
            outv.at[c % OUTV], wgrad_out.at[:, pl.ds(al(c * QCOL, QCOL), QCOL)], out_sem.at[c]
        )

    def t4(c):
        for h in range(2):
            recv(c, h, 6)
            recv(c, h, 7)
        w_now = W.at[c % WBUF]
        pltpu.make_async_copy(w_now, w_now, w_sem.at[c % WBUF]).wait()
        for t in range(MICRO):
            inner[t] += dot(G[c, t].reshape(256, CCOL), W[c % WBUF], ((1,), (1,)))

        @pl.when(c + WBUF < CHUNKS)
        def _():
            w_start(c + WBUF)

        @pl.when(c >= 2)
        def _():
            mate_copy(c - 2).wait_send()

        for cq in range(2):
            for xq in range(2):
                q = xq * 2 + cq
                cols = slice(q * QCOL, (q + 1) * QCOL)
                part = jnp.zeros((512, QCOL), F32)
                for t in range(MICRO):
                    part += dot(
                        gT[:, t * 256 : (t + 1) * 256], G[c, t, :, :, cols].reshape(256, QCOL), ((1,), (0,))
                    )

                @pl.when(core == cq)
                def _():
                    own[c % 2, xq] = part

                @pl.when(core != cq)
                def _():
                    msend[c % 2, xq] = part.astype(BF16)

        mate_copy(c).start()

    def r1(c):
        mate_copy(c).wait_recv()

        @pl.when(c >= 2)
        def _():
            x_copy(c - 2).wait_send()

        @pl.when(c >= OUTV)
        def _():
            out_copy(c - OUTV).wait()

        xsend[c % 2] = (own[c % 2, 1 - xl] + mrecv[c, 1 - xl].astype(F32)).astype(BF16)
        x_copy(c).start()
        outv[c % OUTV] = own[c % 2, xl] + mrecv[c, xl].astype(F32)

    def r2(c):
        x_copy(c).wait_recv()
        outv[c % OUTV] += xrecv[c].astype(F32)
        out_copy(c).start()

    def ra_copy(k, recv):
        dst = RA.at[(d + 4 - k) % 4] if recv else RA.at[d]
        src = dst if recv else RGA.at[(d + k) % 4]
        return remote(src, dst, ra_s.at[k], ra_r.at[k], {"dp": (d + k) % 4})

    def piece(v):
        return pl.ds(al(128 * v, 128), 128)

    def rb_copy(k, recv):
        dst = RBR.at[(tau + 16 - k) % 16] if recv else RBR.at[tau]
        src = dst if recv else RB.at[:, piece((tau + k) % 16)]
        return remote(src, dst, rb_s.at[k], rb_r.at[k], {"tensor": (tau + k) % 16})

    def rc_copy(k, recv):
        dst = RC.at[:, piece((tau + 16 - k) % 16)] if recv else RC.at[:, piece(tau)]
        return remote(dst, dst, rc_s.at[k], rc_r.at[k], {"tensor": (tau + k) % 16})

    def each_peer(fn):
        def go(k, carry):
            fn(k)
            return carry

        lax.fori_loop(1, 16, go, 0)

    def grads_a():
        for k in range(1, 4):
            ra_copy(k, False).start()
        RA[d] = RGA[d]

    def grads_b():
        for k in range(1, 4):
            ra_copy(k, True).wait_recv()
        RB[...] = RA[0] + RA[1] + RA[2] + RA[3]
        each_peer(lambda k: rb_copy(k, False).start())
        RBR[tau] = RB[:, piece(tau)]

    def grads_c():
        each_peer(lambda k: rb_copy(k, True).wait_recv())
        total = RBR[0]
        for k in range(1, 16):
            total += RBR[k]
        RC[:, piece(tau)] = total
        each_peer(lambda k: rc_copy(k, False).start())

    rg_fin = pltpu.make_async_copy(RC, rg_out, fin_sem.at[2])

    def grads_d():
        each_peer(lambda k: rc_copy(k, True).wait_recv())
        rg_fin.start()

    t0(0)
    grads_a()

    def step(s, carry):
        for lag, fn in ((0, t0), (3, t3), (2, t2), (1, t1), (5, r1), (6, r2), (4, t4)):
            low = lag + (1 if fn is t0 else 0)

            @pl.when((s >= low) & (s < CHUNKS + lag))
            def _():
                fn(s - lag)

        @pl.when(s == 1)
        def _():
            dispatch_relay(2)

        for when, fn in ((2, grads_b), (5, grads_c), (8, grads_d)):

            @pl.when(s == when)
            def _():
                fn()

        return carry

    lax.fori_loop(0, CHUNKS + 7, step, 0)

    for t in range(MICRO):
        gate_f = gate_ref[t].astype(F32)
        sig = jax.nn.sigmoid(gate_f)
        rows = inner[t]
        stage[0, t] = (rows * gate_f * sig).astype(BF16)
        stage[1, t] = (rows * scan_ref[t].astype(F32) * sig * (1.0 + gate_f * (1.0 - sig))).astype(BF16)
    fin = [
        pltpu.make_async_copy(stage.at[0], scan_out, fin_sem.at[0]),
        pltpu.make_async_copy(stage.at[1], gate_out, fin_sem.at[1]),
    ]
    for cp in fin:
        cp.start()

    def drain(c, carry):
        for h in range(2):
            for kind in range(8):
                ag_copy(c, h, kind, send_step(kind)).wait_send()
        return carry

    lax.fori_loop(0, CHUNKS, drain, 0)
    for c in range(CHUNKS - OUTV, CHUNKS):
        out_copy(c).wait()
    for c in (CHUNKS - 2, CHUNKS - 1):
        mate_copy(c).wait_send()
        x_copy(c).wait_send()

    def drain_t(t, carry):
        for k in range(1, 4):
            b1_copy(t, k, False).wait_send()
            d2_copy(t, k, True).wait_recv()
        po_copy(t).wait()
        return carry

    lax.fori_loop(0, MICRO, drain_t, 0)
    for t in (1, 2):
        for k in range(1, 4):
            b2_copy(t, k, False).wait_send()
            d1_copy(t, k, False).wait_send()
            d2_copy(t, k, False).wait_send()
        d2_local(t).wait()

    @pl.when(sec == 1)
    def _():
        for t in range(1, MICRO):
            up_copy(t).wait_send()

    for k in range(1, 4):
        rg_copy(k, False).wait_send()
        ra_copy(k, False).wait_send()
    each_peer(lambda k: rb_copy(k, False).wait_send())
    each_peer(lambda k: rc_copy(k, False).wait_send())
    for cp in fin:
        cp.wait()
    rg_fin.wait()


def layer(inc, hid, eo, routes, routes_t, back, scan, gate, weight, rg):
    vmem = pl.BlockSpec(memory_space=pltpu.VMEM)
    hbm = pl.BlockSpec(memory_space=pl.ANY)
    V = pltpu.VMEM
    DMA = pltpu.SemaphoreType.DMA
    return pl.pallas_call(
        layer_kernel,
        out_shape=(
            jax.ShapeDtypeStruct((MICRO, TOK, WIDTH), BF16),
            jax.ShapeDtypeStruct((MICRO, 256, 512), BF16),
            jax.ShapeDtypeStruct((MICRO, 256, 512), BF16),
            jax.ShapeDtypeStruct((MICRO, SLOTS, WIDTH), BF16),
            jax.ShapeDtypeStruct((512, QB), F32),
            jax.ShapeDtypeStruct((24, QB), F32),
        ),
        in_specs=[hbm, vmem, vmem, vmem, vmem, hbm, vmem, vmem, hbm, vmem],
        out_specs=(hbm,) * 6,
        scratch_shapes=[
            V((CHUNKS, MICRO, 4, 64, CCOL), BF16),
            V((WBUF, 512, CCOL), BF16),
            V((512, 768), BF16),
            V((MICRO, 256, 512), F32),
            V((2, 2, 512, QCOL), F32),
            V((OUTV, 512, QCOL), F32),
            V((2, 2, 512, QCOL), BF16),
            V((CHUNKS, 2, 512, QCOL), BF16),
            V((2, 512, QCOL), BF16),
            V((CHUNKS, 512, QCOL), BF16),
            V((2, MICRO, 256, 512), BF16),
            V((MICRO, TOK, WIDTH), BF16),
            V((MICRO, TOK, WIDTH), BF16),
            V((MICRO, TOK, WIDTH), BF16),
            V((4, 32, QB), BF16),
            V((TOK, WIDTH), F32),
            V((4, 24, QB), F32),
            V((4, 24, QB), F32),
            V((24, QB), F32),
            V((16, 24, 128), F32),
            V((24, QB), F32),
            V((MICRO, SLOTS, WIDTH), BF16),
            V((MICRO, SLOTS, WIDTH), BF16),
            V((2, SLOTS, WIDTH), BF16),
            V((2, SLOTS, WIDTH), BF16),
            V((MICRO, SLOTS, WIDTH), BF16),
            V((2, SLOTS, WIDTH), BF16),
            V((MICRO, TOK, EXPERTS), F32),
            V((MICRO, SLOTS, 1), F32),
            V((MICRO, SLOTS, TOK), BF16),
            V((MICRO, TOK, SLOTS), BF16),
            V((MICRO, TOK, 1), F32),
            DMA((CHUNKS, 2, 8)),
            DMA((CHUNKS, 2, 8)),
            DMA((WBUF,)),
            DMA((CHUNKS,)),
            DMA((CHUNKS,)),
            DMA((CHUNKS,)),
            DMA((CHUNKS,)),
            DMA((CHUNKS,)),
            DMA((3,)),
            DMA((MICRO,)),
        ]
        + [DMA((MICRO, 4))] * 8
        + [DMA((4,))] * 2
        + [DMA((MICRO,))] * 3
        + [DMA((4,))] * 2
        + [DMA((16,))] * 4,
        compiler_params=pltpu.CompilerParams(
            collective_id=0, has_side_effects=True, vmem_limit_bytes=63 * 1024 * 1024
        ),
        cost_estimate=pl.CostEstimate(flops=14_000_000_000, bytes_accessed=30_000_000, transcendentals=0),
    )(inc, hid, eo, routes, routes_t, back, scan, gate, weight, rg)


def on_device(
    incoming, hidden, expert_out, routes, expert_back, scan_out, gate_in, w_out, w_router, norm_gain
):
    rg = jnp.concatenate(
        [w_router[0].T, norm_gain, jnp.zeros((15, w_router.shape[1]), w_router.dtype)], axis=0
    )
    eo = expert_out[0].reshape(MICRO, 2 * TOK, WIDTH)
    passed, scan_grad, gate_grad, expert_grad, weight_grad, small = layer(
        incoming[0], hidden[0], eo, routes[0], jnp.swapaxes(routes[0], 1, 2), expert_back[0],
        scan_out[0], gate_in[0], w_out[0], rg,
    )
    return (
        passed[None],
        scan_grad[None],
        gate_grad[None],
        expert_grad[None],
        weight_grad[None],
        small[:EXPERTS].T[None],
        small[EXPERTS : EXPERTS + 1],
    )


def solution(mesh):
    placed = (
        P("section", None, ("dp", "tensor"), None),
        P("section", None, ("dp", "tensor"), None),
        P("section", None, ("dp", "tensor"), None, None),
        P("section", None, ("dp", "tensor"), None),
        P("section", None, ("dp", "tensor"), None),
        P("section", None, "dp", "tensor"),
        P("section", None, "dp", "tensor"),
        P("section", "tensor", None),
        P("section", "dp", None),
        P("section", "dp"),
    )
    return jax.shard_map(
        on_device,
        mesh=mesh,
        in_specs=placed,
        out_specs=(
            P("section", None, ("dp", "tensor"), None),
            P("section", None, "dp", "tensor"),
            P("section", None, "dp", "tensor"),
            P("section", None, ("dp", "tensor"), None),
            P("section", "tensor", "dp"),
            P("section", "dp", None),
            P("section", "dp"),
        ),
        check_vma=False,
    )
```

time: 370 us -> 221 us (0.60)
  Pallas kernels: 113 us -> 199 us
  waiting for transfers between devices: 59.2 us -> 0 us
  blocking collectives: 53.2 us -> 0 us
  starting transfers between devices: 41.8 us -> 0 us
  other arithmetic: 29.4 us -> 1.59 us
  local copies, waits for them, and re-layouts: 43.1 us -> 19.8 us
  between operations: 15.3 us -> 0.66 us
  matrix products: 12.8 us -> 0 us
    pallas_call x1, Pallas kernels: 113 us -> 199 us  [layer(): pl.pallas_call(layer_kernel, out_shape=(jax.ShapeDtypeStruct((MICRO, TOK,...]
    all_to_all x6 -> x0, starting transfers between devices: 38.7 us -> none  [the longest x3 20 us: on_device(): lax.all_to_all(expert_back[0, micro_step], 'tensor', split_axis=0, concat...]
    psum x1 -> x0, waiting for transfers between devices: 34.5 us -> none  [on_device(): lax.psum(router_acc.astype(jnp.bfloat16), 'tensor').astype(jnp.float32)]
    psum x1 -> x0, blocking collectives: 31.5 us -> none  [on_device(): lax.psum(gain_acc.astype(jnp.bfloat16), 'tensor').astype(jnp.float32)]
    all_to_all x6 -> x0, waiting for transfers between devices: 16.9 us -> none  [the longest x3 15.8 us: on_device(): lax.all_to_all(expert_back[0, micro_step], 'tensor', split_axis=0, concat...]
    dot_general x12 -> x0, matrix products: 12.8 us -> none  [the longest x3 7.54 us: on_device(): jnp.einsum('td,tkd->tk', upstream, expert_out[0, micro_step], preferred_e...]
    all_gather x2 -> x0, blocking collectives: 11.8 us -> none  [the longest x1 5.95 us: on_device(): lax.all_gather(norm_gain[0], 'dp', axis=0, tiled=True)]
    all_to_all x9 -> x0, local copies, waits for them, and re-layouts: 11.2 us -> none  [the longest x6 6.55 us: on_device(): lax.all_to_all(expert_back[0, micro_step], 'tensor', split_axis=0, concat...]
  transfers between devices with their start and end apart: 10 -> 0, of which waited for: 4 -> 0; matrix products, arithmetic and copies ran while one was open for 15% -> 0% of each run, Pallas kernels for 31% -> 0%
where the time goes in v1:
time: 221 us
  Pallas kernels  199 us (90%)
  local copies, waits for them, and re-layouts  19.8 us (9%)
    pallas_call x1, Pallas kernels, layer(): pl.pallas_call(layer_kernel, out_shape=(jax.ShapeDtypeStruct((MICRO, TOK,...  199 us
    unnamed x9, local copies, waits for them, and re-layouts  11.5 us

profile of v1, /device:TPU:1, one launch (start us, length us, event | category | flops | bytes accessed | tf_op | source)
XLA Modules:
  0.0 220.7 jit_solution(11866703787709279462)
XLA Ops:
  0.6 0.1 pad.2.clone
  0.7 1.4 copy.17.routes_ref
  2.1 1.6 maximum_maximum_fusion.rg_ref
  3.7 3.6 %reshape_squeeze.3.eo_ref = bf16[3,32,8192]{2,1,0:T(8,128)(2,1)} reshape(bf16[1,3,16,2,8192]{4,3,2,1,0:T(2,128)(2,1)} %param.12) | data formatting | bytes 3145728 | tf_op jit(solution)/shard_map/reshape;squeeze | solution.py:700
  7.3 198.7 %shard_map.153 = (bf16[3,16,8192]{2,1,0:T(8,128)(2,1)}, bf16[3,256,512]{2,1,0:T(8,128)(2,1)}, bf16[3,256,512]{2,1,0:T(8,128)(2,1)}, bf16[3,64,8192]{2,1,0:T(8,12...) custom-call(bf16[3,16,8192]{2,1,0:T(8,128)(2,1)} %bitcast.31, bf16[3,16,8192]{2,1,0:T(8,128)(2,1)} %bitcast.32, ...), custom_call_target="tpu_custom_call" | custom-call | flops 14000000000 | bytes 30000000 | tf_op jit(solution)/shard_map/pallas_call | solution.py:626
  206.0 0.0 copy-start.1
  206.0 1.6 slice.7
  207.6 1.6 slice_bitcast_fusion
  209.2 2.1 copy.23
  211.2 2.1 copy.24
  213.3 2.1 copy.25
  215.4 0.0 copy-done.1
  215.4 0.0 copy-start
  215.4 1.7 copy.26
  217.0 1.7 copy-done
  218.7 2.0 copy.27
  (1 shorter events, 0.0 us)
Async XLA Ops:
  206.0 9.4 %copy-start.1 = (bf16[3,64,8192]{2,1,0:T(8,128)(2,1)S(1)}, bf16[3,64,8192]{2,1,0:T(8,128)(2,1)}, u32[]{:S(2)}) copy-start(bf16[3,64,8192]{2,1,0:T(8,128)(2,1)} %get-tuple-element.16) | copy-start | bytes 9437188
  215.4 3.3 %copy-start = (f32[512,2048]{1,0:T(8,128)S(1)}, f32[512,2048]{1,0:T(8,128)}, u32[]{:S(2)}) copy-start(f32[512,2048]{1,0:T(8,128)} %get-tuple-element.17) | copy-start | bytes 12582916

commit v2 on v1

--- a/solution.py
+++ b/solution.py
@@ -31,10 +31,12 @@
 
 
 def layer_kernel(
-    inc_hbm, hid_ref, eo_ref, routes_ref, routes_t_ref, back_hbm, scan_ref, gate_ref, w_hbm, rg_ref,
+    inc_hbm, hid_hbm, eo_hbm, routes_t_ref, back_hbm, scan_hbm, gate_hbm, w_hbm, wr_ref, gain_ref,
     passed_out, scan_out, gate_out, exp_out, wgrad_out, rg_out,
     G, W, gT, inner, own, outv, msend, mrecv, xsend, xrecv, stage,
     UP, PO, NR, RG, NG, RGA, RA, RB, RBR, RC, BR1, BR2, BP, DS, DR, DP,
+    hid_ref, eo_ref, scan_ref, gate_ref, in_sem,
+    fw_b1, fw_b2, fw_d1, fw_d2, own_b, own_d,
     probs_s, prob64_s, sel_s, selb_s, inv_s,
     ag_s, ag_r, w_sem, ms_s, ms_r, xs_s, xs_r, out_sem, fin_sem, po_sem,
     b1_s, b1_r, b2_s, b2_r, d1_s, d1_r, d2_s, d2_r, rg_s, rg_r, up_l, up_s, up_r,
@@ -78,6 +80,19 @@
         pl.semaphore_signal(barrier, inc=1, device_id={"dp": (d + k) % 4}, device_id_type=MESH)
     pl.semaphore_signal(barrier, inc=1, device_id={"section": 1 - sec}, device_id_type=MESH)
 
+    loads = [
+        pltpu.make_async_copy(src, dst, in_sem.at[n])
+        for n, (src, dst) in enumerate(
+            ((hid_hbm, hid_ref), (eo_hbm, eo_ref), (scan_hbm, scan_ref), (gate_hbm, gate_ref))
+        )
+    ]
+    for cp in loads:
+        cp.start()
+    RG[d, 0:EXPERTS, :] = wr_ref[...]
+    RG[d, EXPERTS : 2 * EXPERTS, :] = jnp.broadcast_to(
+        gain_ref[...].astype(F32), (EXPERTS, QB)
+    ).astype(BF16)
+
     def up_local(t):
         return pltpu.make_async_copy(inc_hbm.at[t], UP.at[t], up_l.at[t])
 
@@ -96,63 +111,88 @@
                 w_sem.at[c % WBUF],
             ).start()
 
-    def b1_copy(t, k, recv):
-        if recv:
-            ref = BR1.at[t, rows16((z + 4 - k) % 4)]
-            return remote(ref, ref, b1_s.at[t, k], b1_r.at[t, k], {"tensor": at_z(k)})
-        return remote(
-            back_hbm.at[t, rows16((z + k) % 4)], BR1.at[t, rows16(z)],
-            b1_s.at[t, k], b1_r.at[t, k], {"tensor": at_z(k)},
-        )
+    class Exchange:
+        def __init__(self, src, dst, nbr, coord, fw, ss, rs):
+            self.src, self.dst, self.nbr, self.coord = src, dst, nbr, coord
+            self.fw, self.ss, self.rs = fw, ss, rs
+
+        def at(self, t, kind, recv):
+            def v(k):
+                return (self.coord + k) % 4
+
+            low, high, whole = pl.ds(0, WIDTH // 2), pl.ds(WIDTH // 2, WIDTH // 2), pl.ds(0, WIDTH)
+            half = (low, high)[kind % 2]
+            if kind < 2:
+                target = self.fw.at[t, kind]
+                source = target if recv else self.src(t, v(2), half)
+            elif kind < 4:
+                target = self.dst(t, v(3 if kind == 2 else 1) if recv else self.coord, whole)
+                source = target if recv else self.src(t, v(1 if kind == 2 else 3), whole)
+            else:
+                target = self.dst(t, v(2) if recv else v(3 if kind == 4 else 1), half)
+                source = target if recv else self.fw.at[t, kind - 4]
+            return remote(
+                source, target, self.ss.at[t, kind], self.rs.at[t, kind],
+                {"tensor": self.nbr(1 if kind % 2 == 0 else 3)},
+            )
+
+        def start(self, t):
+            for kind in range(4):
+                self.at(t, kind, False).start()
+
+        def forward(self, t):
+            for kind in range(2):
+                self.at(t, kind, True).wait_recv()
+                self.at(t, kind + 4, False).start()
+
+        def arrived(self, t):
+            for kind in range(2, 6):
+                self.at(t, kind, True).wait_recv()
+
+        def sent(self, t):
+            for kind in range(4):
+                self.at(t, kind, False).wait_send()
+
+        def passed_on(self, t):
+            for kind in (4, 5):
+                self.at(t, kind, False).wait_send()
+
+    b1 = Exchange(
+        lambda t, v, cols: back_hbm.at[t, rows16(v), cols], lambda t, v, cols: BR1.at[t, rows16(v), cols],
+        at_z, z, fw_b1, b1_s, b1_r,
+    )
+    b2 = Exchange(
+        lambda t, v, cols: BP.at[t % 2, rows16(v), cols], lambda t, v, cols: BR2.at[t, rows16(v), cols],
+        at_y, y, fw_b2, b2_s, b2_r,
+    )
+    d1 = Exchange(
+        lambda t, v, cols: DS.at[t % 2, rows16(v), cols], lambda t, v, cols: DR.at[t, rows16(v), cols],
+        at_y, y, fw_d1, d1_s, d1_r,
+    )
+    d2 = Exchange(
+        lambda t, v, cols: DP.at[t % 2, rows16(v), cols], lambda t, v, cols: exp_out.at[t, rows16(v), cols],
+        at_z, z, fw_d2, d2_s, d2_r,
+    )
 
     def b1_local(t):
-        return pltpu.make_async_copy(back_hbm.at[t, rows16(z)], BR1.at[t, rows16(z)], b1_r.at[t, 0])
-
-    def b2_copy(t, k, recv):
-        if recv:
-            ref = BR2.at[t, rows16((y + 4 - k) % 4)]
-            return remote(ref, ref, b2_s.at[t, k], b2_r.at[t, k], {"tensor": at_y(k)})
-        return remote(
-            BP.at[t % 2, rows16((y + k) % 4)], BR2.at[t, rows16(y)],
-            b2_s.at[t, k], b2_r.at[t, k], {"tensor": at_y(k)},
-        )
-
-    def d1_copy(t, k, recv):
-        if recv:
-            ref = DR.at[t, rows16((y + 4 - k) % 4)]
-            return remote(ref, ref, d1_s.at[t, k], d1_r.at[t, k], {"tensor": at_y(k)})
-        return remote(
-            DS.at[t % 2, rows16((y + k) % 4)], DR.at[t, rows16(y)],
-            d1_s.at[t, k], d1_r.at[t, k], {"tensor": at_y(k)},
-        )
-
-    def d2_copy(t, k, recv):
-        if recv:
-            ref = exp_out.at[t, rows16((z + 4 - k) % 4)]
-            return remote(ref, ref, d2_s.at[t, k], d2_r.at[t, k], {"tensor": at_z(k)})
-        return remote(
-            DP.at[t % 2, rows16((z + k) % 4)], exp_out.at[t, rows16(z)],
-            d2_s.at[t, k], d2_r.at[t, k], {"tensor": at_z(k)},
-        )
+        return pltpu.make_async_copy(back_hbm.at[t, rows16(z)], BR1.at[t, rows16(z)], own_b.at[t])
 
     def d2_local(t):
-        return pltpu.make_async_copy(DP.at[t % 2, rows16(z)], exp_out.at[t, rows16(z)], d2_r.at[t, 0])
+        return pltpu.make_async_copy(DP.at[t % 2, rows16(z)], exp_out.at[t, rows16(z)], own_d.at[t])
 
     def rg_copy(k, recv):
         ref = RG.at[(d + 4 - k) % 4] if recv else RG.at[d]
-        return remote(ref if recv else rg_ref, ref, rg_s.at[k], rg_r.at[k], {"dp": (d + k) % 4})
+        return remote(ref, ref, rg_s.at[k], rg_r.at[k], {"dp": (d + k) % 4})
 
     pl.semaphore_wait(barrier, 19)
 
     for k in range(1, 4):
         rg_copy(k, False).start()
     for t in range(MICRO):
-        for k in (2, 1, 3):
-            b1_copy(t, k, False).start()
+        b1.start(t)
         b1_local(t).start()
     for c in range(WBUF):
         w_start(c)
-    RG[d] = rg_ref[...]
 
     slot_r = iota((SLOTS, TOK), 0)
     slot_e = ((slot_r >> 2) & 3) * 4 + (slot_r >> 4)
@@ -165,6 +205,12 @@
     perm = (perm_in == ((perm_out >> 2) & 3) * 16 + (perm_out >> 4) * 4 + (perm_out & 3)).astype(F32).astype(BF16)
     upper = (iota((TOK, TOK), 0) < iota((TOK, TOK), 1)).astype(F32).astype(BF16)
     lower = (iota((TOK, TOK), 0) > iota((TOK, TOK), 1)).astype(F32).astype(BF16)
+
+    eye = iota((TOK, TOK), 0) == iota((TOK, TOK), 1)
+
+    def route_col(t, k):
+        row = routes_t_ref[t, k : k + 1, :].astype(F32)
+        return jnp.sum(jnp.where(eye, row, 0.0), axis=1, keepdims=True).astype(jnp.int32)
 
     RGA[...] = jnp.zeros_like(RGA)
     for k in range(1, 4):
@@ -205,62 +251,57 @@
         sel = jnp.where(before == slot_c.astype(F32), named, 0.0)
         sel_s[t] = sel.astype(BF16)
         prob64_s[t] = jnp.sum(sel * spread, axis=1, keepdims=True)
-        r0 = routes_ref[t, :, 0:1]
-        r1 = routes_ref[t, :, 1:2]
+        r0 = route_col(t, 0)
+        r1 = route_col(t, 1)
         named_b = ((r0 == slot_eb) | (r1 == slot_eb)).astype(F32)
         before_b = dot(lower, named_b.astype(BF16), ((1,), (0,)))
         selb_s[t] = jnp.where(before_b == slot_cb.astype(F32), named_b, 0.0).astype(BF16)
         return carry
 
+    loads[0].wait()
     lax.fori_loop(0, MICRO, prepare, 0)
+    for cp in loads[1:]:
+        cp.wait()
 
     def dispatch(t):
         @pl.when(t >= 2)
         def _():
-            for k in range(1, 4):
-                d1_copy(t - 2, k, False).wait_send()
+            d1.sent(t - 2)
 
         prob = prob64_s[t]
         sel = sel_s[t]
         for q in range(4):
             cols = slice(q * QB, (q + 1) * QB)
             DS[t % 2, :, cols] = (dot(sel, UP[t, :, cols], ((1,), (0,))) * prob).astype(BF16)
-        for k in (2, 1, 3):
-            d1_copy(t, k, False).start()
+        d1.start(t)
         DR[t, rows16(y), :] = DS[t % 2, rows16(y), :]
 
     def dispatch_relay(t):
-        for k in range(1, 4):
-            d1_copy(t, k, True).wait_recv()
+        d1.arrived(t)
 
         @pl.when(t >= 2)
         def _():
-            for k in range(1, 4):
-                d2_copy(t - 2, k, False).wait_send()
+            d2.sent(t - 2)
             d2_local(t - 2).wait()
 
         for q in range(4):
             cols = slice(q * QB, (q + 1) * QB)
             DP[t % 2, :, cols] = dot(perm, DR[t, :, cols], ((1,), (0,))).astype(BF16)
-        for k in (2, 1, 3):
-            d2_copy(t, k, False).start()
+        d2.start(t)
         d2_local(t).start()
 
     def back_relay(t):
-        for k in range(1, 4):
-            b1_copy(t, k, True).wait_recv()
+        b1.arrived(t)
         b1_local(t).wait()
 
         @pl.when(t >= 2)
         def _():
-            for k in range(1, 4):
-                b2_copy(t - 2, k, False).wait_send()
+            b2.sent(t - 2)
 
         for q in range(4):
             cols = slice(q * QB, (q + 1) * QB)
             BP[t % 2, :, cols] = dot(perm, BR1[t, :, cols], ((1,), (0,))).astype(BF16)
-        for k in (2, 1, 3):
-            b2_copy(t, k, False).start()
+        b2.start(t)
         BR2[t, rows16(y), :] = BP[t % 2, rows16(y), :]
 
     def up_copy(t):
@@ -279,19 +320,18 @@
             up_copy(t).wait_recv()
 
     def combine(t):
-        for k in range(1, 4):
-            b2_copy(t, k, True).wait_recv()
+        b2.arrived(t)
         scores = jnp.zeros((TOK, 2 * TOK), F32)
         for q in range(4):
             cols = slice(q * QB, (q + 1) * QB)
-            scores += dot(UP[t, :, cols], eo_ref[t, :, cols], ((1,), (1,)))
+            scores += dot(UP[t, :, cols], eo_ref[t, :, :, cols].reshape(2 * TOK, QB), ((1,), (1,)))
         row_i = iota((TOK, 2 * TOK), 0)
         col_i = iota((TOK, 2 * TOK), 1)
         s0 = jnp.sum(jnp.where(col_i == 2 * row_i, scores, 0.0), axis=1, keepdims=True)
         s1 = jnp.sum(jnp.where(col_i == 2 * row_i + 1, scores, 0.0), axis=1, keepdims=True)
         expert_i = iota((TOK, EXPERTS), 1)
-        prob_grad = jnp.where(routes_ref[t, :, 0:1] == expert_i, s0, 0.0) + jnp.where(
-            routes_ref[t, :, 1:2] == expert_i, s1, 0.0
+        prob_grad = jnp.where(route_col(t, 0) == expert_i, s0, 0.0) + jnp.where(
+            route_col(t, 1) == expert_i, s1, 0.0
         )
         probs = probs_s[t]
         logit_grad = (
@@ -334,7 +374,27 @@
 
         @pl.when(s < MICRO)
         def _():
+            b1.forward(s)
+
+        @pl.when(s >= 1)
+        def _():
+            b2.forward(s - 1)
+
+        @pl.when(s < MICRO)
+        def _():
             back_relay(s)
+
+        @pl.when(s == 0)
+        def _():
+            d1.forward(0)
+
+        @pl.when(s == 2)
+        def _():
+            d2.forward(0)
+
+        @pl.when(s == 3)
+        def _():
+            d1.forward(1)
 
         @pl.when(s >= 1)
         def _():
@@ -550,7 +610,16 @@
 
         @pl.when(s == 1)
         def _():
+            d1.forward(2)
+            d2.forward(1)
+
+        @pl.when(s == 2)
+        def _():
             dispatch_relay(2)
+
+        @pl.when(s == 4)
+        def _():
+            d2.forward(2)
 
         for when, fn in ((2, grads_b), (5, grads_c), (8, grads_d)):
 
@@ -589,18 +658,18 @@
         x_copy(c).wait_send()
 
     def drain_t(t, carry):
-        for k in range(1, 4):
-            b1_copy(t, k, False).wait_send()
-            d2_copy(t, k, True).wait_recv()
+        b1.sent(t)
+        d2.arrived(t)
+        for ex in (b1, b2, d1, d2):
+            ex.passed_on(t)
         po_copy(t).wait()
         return carry
 
     lax.fori_loop(0, MICRO, drain_t, 0)
     for t in (1, 2):
-        for k in range(1, 4):
-            b2_copy(t, k, False).wait_send()
-            d1_copy(t, k, False).wait_send()
-            d2_copy(t, k, False).wait_send()
+        b2.sent(t)
+        d1.sent(t)
+        d2.sent(t)
         d2_local(t).wait()
 
     @pl.when(sec == 1)
@@ -618,7 +687,7 @@
     rg_fin.wait()
 
 
-def layer(inc, hid, eo, routes, routes_t, back, scan, gate, weight, rg):
+def layer(inc, hid, eo, routes_t, back, scan, gate, weight, router, gain):
     vmem = pl.BlockSpec(memory_space=pltpu.VMEM)
     hbm = pl.BlockSpec(memory_space=pl.ANY)
     V = pltpu.VMEM
@@ -633,7 +702,7 @@
             jax.ShapeDtypeStruct((512, QB), F32),
             jax.ShapeDtypeStruct((24, QB), F32),
         ),
-        in_specs=[hbm, vmem, vmem, vmem, vmem, hbm, vmem, vmem, hbm, vmem],
+        in_specs=[hbm, hbm, hbm, vmem, hbm, hbm, hbm, hbm, vmem, vmem],
         out_specs=(hbm,) * 6,
         scratch_shapes=[
             V((CHUNKS, MICRO, 4, 64, CCOL), BF16),
@@ -663,6 +732,17 @@
             V((2, SLOTS, WIDTH), BF16),
             V((MICRO, SLOTS, WIDTH), BF16),
             V((2, SLOTS, WIDTH), BF16),
+            V((MICRO, TOK, WIDTH), BF16),
+            V((MICRO, TOK, 2, WIDTH), BF16),
+            V((MICRO, 256, 512), BF16),
+            V((MICRO, 256, 512), BF16),
+            DMA((4,)),
+            V((MICRO, 2, TOK, WIDTH // 2), BF16),
+            V((MICRO, 2, TOK, WIDTH // 2), BF16),
+            V((MICRO, 2, TOK, WIDTH // 2), BF16),
+            V((MICRO, 2, TOK, WIDTH // 2), BF16),
+            DMA((MICRO,)),
+            DMA((MICRO,)),
             V((MICRO, TOK, EXPERTS), F32),
             V((MICRO, SLOTS, 1), F32),
             V((MICRO, SLOTS, TOK), BF16),
@@ -679,7 +759,7 @@
             DMA((3,)),
             DMA((MICRO,)),
         ]
-        + [DMA((MICRO, 4))] * 8
+        + [DMA((MICRO, 6))] * 8
         + [DMA((4,))] * 2
         + [DMA((MICRO,))] * 3
         + [DMA((4,))] * 2
@@ -688,28 +768,51 @@
             collective_id=0, has_side_effects=True, vmem_limit_bytes=63 * 1024 * 1024
         ),
         cost_estimate=pl.CostEstimate(flops=14_000_000_000, bytes_accessed=30_000_000, transcendentals=0),
-    )(inc, hid, eo, routes, routes_t, back, scan, gate, weight, rg)
+    )(inc, hid, eo, routes_t, back, scan, gate, weight, router, gain)
+
+
+def finish_kernel(*refs):
+    sems = refs[-1]
+    small, router, gain = refs[5], refs[11], refs[12]
+    copies = [pltpu.make_async_copy(refs[n], refs[6 + n], sems.at[n]) for n in range(5)]
+    for cp in copies:
+        cp.start()
+    router[...] = small[0:EXPERTS, :]
+    gain[...] = small[EXPERTS : EXPERTS + 1, :]
+    for cp in copies:
+        cp.wait()
+
+
+def finish(arrays):
+    vmem = pl.BlockSpec(memory_space=pltpu.VMEM)
+    hbm = pl.BlockSpec(memory_space=pl.ANY)
+    return pl.pallas_call(
+        finish_kernel,
+        out_shape=tuple(jax.ShapeDtypeStruct(a.shape, a.dtype) for a in arrays[:5])
+        + (jax.ShapeDtypeStruct((EXPERTS, QB), F32), jax.ShapeDtypeStruct((1, QB), F32)),
+        in_specs=[hbm] * 5 + [vmem],
+        out_specs=(hbm,) * 5 + (vmem, vmem),
+        scratch_shapes=[pltpu.SemaphoreType.DMA((5,))],
+        cost_estimate=pl.CostEstimate(flops=0, bytes_accessed=20_000_000, transcendentals=0),
+    )(*arrays)
 
 
 def on_device(
     incoming, hidden, expert_out, routes, expert_back, scan_out, gate_in, w_out, w_router, norm_gain
 ):
-    rg = jnp.concatenate(
-        [w_router[0].T, norm_gain, jnp.zeros((15, w_router.shape[1]), w_router.dtype)], axis=0
+    outs = layer(
+        incoming[0], hidden[0], expert_out[0], jnp.swapaxes(routes[0], 1, 2), expert_back[0],
+        scan_out[0], gate_in[0], w_out[0], w_router[0].T, norm_gain,
     )
-    eo = expert_out[0].reshape(MICRO, 2 * TOK, WIDTH)
-    passed, scan_grad, gate_grad, expert_grad, weight_grad, small = layer(
-        incoming[0], hidden[0], eo, routes[0], jnp.swapaxes(routes[0], 1, 2), expert_back[0],
-        scan_out[0], gate_in[0], w_out[0], rg,
-    )
+    passed, scan_grad, gate_grad, expert_grad, weight_grad, router, gain = finish(outs)
     return (
         passed[None],
         scan_grad[None],
         gate_grad[None],
         expert_grad[None],
         weight_grad[None],
-        small[:EXPERTS].T[None],
-        small[EXPERTS : EXPERTS + 1],
+        router.T[None],
+        gain,
     )
 
 

time: 221 us -> 509 us (2.30)
  Pallas kernels: 199 us -> 507 us
  local copies, waits for them, and re-layouts: 19.8 us -> 0 us
    pallas_call x0 -> x1, Pallas kernels: none -> 297 us  [finish(): pl.pallas_call(finish_kernel, out_shape=tuple((jax.ShapeDtypeStruct(a.sha...]
    pallas_call x1, Pallas kernels: 199 us -> 210 us  [layer(): pl.pallas_call(layer_kernel, out_shape=(jax.ShapeDtypeStruct((MICRO, TOK,...]
    unnamed x9 -> x0, local copies, waits for them, and re-layouts: 11.5 us -> none
where the time goes in v2:
time: 509 us; the launch traced here: 508 us
  Pallas kernels  507 us (100%)
    pallas_call x1, Pallas kernels, finish(): pl.pallas_call(finish_kernel, out_shape=tuple((jax.ShapeDtypeStruct(a.sha...  297 us
    pallas_call x1, Pallas kernels, layer(): pl.pallas_call(layer_kernel, out_shape=(jax.ShapeDtypeStruct((MICRO, TOK,...  210 us

profile of v2, /device:TPU:1, one launch (start us, length us, event | category | flops | bytes accessed | tf_op | source)
XLA Modules:
  0.0 507.6 jit_solution(1656707758774515817)
XLA Ops:
  0.6 210.5 %shard_map.153 = (bf16[3,16,8192]{2,1,0:T(8,128)(2,1)}, bf16[3,256,512]{2,1,0:T(8,128)(2,1)}, bf16[3,256,512]{2,1,0:T(8,128)(2,1)}, bf16[3,64,8192]{2,1,0:T(8,12...) custom-call(bf16[3,16,8192]{2,1,0:T(8,128)(2,1)} %bitcast.26, bf16[3,16,8192]{2,1,0:T(8,128)(2,1)} %bitcast.27, ...), custom_call_target="tpu_custom_call" | custom-call | flops 14000000000 | bytes 30000000 | tf_op jit(solution)/shard_map/pallas_call | solution.py:695
  211.1 296.6 %shard_map.154 = (bf16[3,16,8192]{2,1,0:T(8,128)(2,1)}, bf16[3,256,512]{2,1,0:T(8,128)(2,1)}, bf16[3,256,512]{2,1,0:T(8,128)(2,1)}, bf16[3,64,8192]{2,1,0:T(8,12...) custom-call(bf16[3,16,8192]{2,1,0:T(8,128)(2,1)} %get-tuple-element.20.refs_0_, ...), custom_call_target="tpu_custom_call" | custom-call | bytes 20000000 | tf_op jit(solution)/shard_map/pallas_call | solution.py:789

commit v3 on v1

--- a/solution.py
+++ b/solution.py
@@ -17,7 +17,7 @@
 CCOL = 1024
 HALF = 512
 OUTV = 4
-WBUF = 3
+WBUF = 2
 F32 = jnp.float32
 BF16 = jnp.bfloat16
 
@@ -31,10 +31,12 @@
 
 
 def layer_kernel(
-    inc_hbm, hid_ref, eo_ref, routes_ref, routes_t_ref, back_hbm, scan_ref, gate_ref, w_hbm, rg_ref,
+    inc_hbm, hid_hbm, eo_hbm, routes_t_ref, back_hbm, scan_hbm, gate_hbm, w_hbm, wr_ref, gain_ref,
     passed_out, scan_out, gate_out, exp_out, wgrad_out, rg_out,
     G, W, gT, inner, own, outv, msend, mrecv, xsend, xrecv, stage,
     UP, PO, NR, RG, NG, RGA, RA, RB, RBR, RC, BR1, BR2, BP, DS, DR, DP,
+    hid_ref, eo_ref, scan_ref, gate_ref, in_sem,
+    EB, DX, eb_sem, dx_sem,
     probs_s, prob64_s, sel_s, selb_s, inv_s,
     ag_s, ag_r, w_sem, ms_s, ms_r, xs_s, xs_r, out_sem, fin_sem, po_sem,
     b1_s, b1_r, b2_s, b2_r, d1_s, d1_r, d2_s, d2_r, rg_s, rg_r, up_l, up_s, up_r,
@@ -78,6 +80,20 @@
         pl.semaphore_signal(barrier, inc=1, device_id={"dp": (d + k) % 4}, device_id_type=MESH)
     pl.semaphore_signal(barrier, inc=1, device_id={"section": 1 - sec}, device_id_type=MESH)
 
+    loads = [
+        pltpu.make_async_copy(src, dst, in_sem.at[n])
+        for n, (src, dst) in enumerate(
+            ((hid_hbm, hid_ref), (eo_hbm, eo_ref), (scan_hbm, scan_ref), (gate_hbm, gate_ref))
+        )
+    ]
+    eb_loads = [pltpu.make_async_copy(back_hbm.at[t], EB.at[t], eb_sem.at[t]) for t in range(MICRO)]
+    for cp in eb_loads + loads:
+        cp.start()
+    RG[d, 0:EXPERTS, :] = wr_ref[...]
+    RG[d, EXPERTS : 2 * EXPERTS, :] = jnp.broadcast_to(
+        gain_ref[...].astype(F32), (EXPERTS, QB)
+    ).astype(BF16)
+
     def up_local(t):
         return pltpu.make_async_copy(inc_hbm.at[t], UP.at[t], up_l.at[t])
 
@@ -101,12 +117,12 @@
             ref = BR1.at[t, rows16((z + 4 - k) % 4)]
             return remote(ref, ref, b1_s.at[t, k], b1_r.at[t, k], {"tensor": at_z(k)})
         return remote(
-            back_hbm.at[t, rows16((z + k) % 4)], BR1.at[t, rows16(z)],
+            EB.at[t, rows16((z + k) % 4)], BR1.at[t, rows16(z)],
             b1_s.at[t, k], b1_r.at[t, k], {"tensor": at_z(k)},
         )
 
     def b1_local(t):
-        return pltpu.make_async_copy(back_hbm.at[t, rows16(z)], BR1.at[t, rows16(z)], b1_r.at[t, 0])
+        return pltpu.make_async_copy(EB.at[t, rows16(z)], BR1.at[t, rows16(z)], b1_r.at[t, 0])
 
     def b2_copy(t, k, recv):
         if recv:
@@ -128,31 +144,31 @@
 
     def d2_copy(t, k, recv):
         if recv:
-            ref = exp_out.at[t, rows16((z + 4 - k) % 4)]
+            ref = DX.at[t, rows16((z + 4 - k) % 4)]
             return remote(ref, ref, d2_s.at[t, k], d2_r.at[t, k], {"tensor": at_z(k)})
         return remote(
-            DP.at[t % 2, rows16((z + k) % 4)], exp_out.at[t, rows16(z)],
+            DP.at[t % 2, rows16((z + k) % 4)], DX.at[t, rows16(z)],
             d2_s.at[t, k], d2_r.at[t, k], {"tensor": at_z(k)},
         )
 
     def d2_local(t):
-        return pltpu.make_async_copy(DP.at[t % 2, rows16(z)], exp_out.at[t, rows16(z)], d2_r.at[t, 0])
+        return pltpu.make_async_copy(DP.at[t % 2, rows16(z)], DX.at[t, rows16(z)], d2_r.at[t, 0])
 
     def rg_copy(k, recv):
         ref = RG.at[(d + 4 - k) % 4] if recv else RG.at[d]
-        return remote(ref if recv else rg_ref, ref, rg_s.at[k], rg_r.at[k], {"dp": (d + k) % 4})
+        return remote(ref, ref, rg_s.at[k], rg_r.at[k], {"dp": (d + k) % 4})
 
     pl.semaphore_wait(barrier, 19)
 
     for k in range(1, 4):
         rg_copy(k, False).start()
     for t in range(MICRO):
+        eb_loads[t].wait()
         for k in (2, 1, 3):
             b1_copy(t, k, False).start()
         b1_local(t).start()
     for c in range(WBUF):
         w_start(c)
-    RG[d] = rg_ref[...]
 
     slot_r = iota((SLOTS, TOK), 0)
     slot_e = ((slot_r >> 2) & 3) * 4 + (slot_r >> 4)
@@ -165,6 +181,12 @@
     perm = (perm_in == ((perm_out >> 2) & 3) * 16 + (perm_out >> 4) * 4 + (perm_out & 3)).astype(F32).astype(BF16)
     upper = (iota((TOK, TOK), 0) < iota((TOK, TOK), 1)).astype(F32).astype(BF16)
     lower = (iota((TOK, TOK), 0) > iota((TOK, TOK), 1)).astype(F32).astype(BF16)
+
+    eye = iota((TOK, TOK), 0) == iota((TOK, TOK), 1)
+
+    def route_col(t, k):
+        row = routes_t_ref[t, k : k + 1, :].astype(F32)
+        return jnp.sum(jnp.where(eye, row, 0.0), axis=1, keepdims=True).astype(jnp.int32)
 
     RGA[...] = jnp.zeros_like(RGA)
     for k in range(1, 4):
@@ -205,14 +227,17 @@
         sel = jnp.where(before == slot_c.astype(F32), named, 0.0)
         sel_s[t] = sel.astype(BF16)
         prob64_s[t] = jnp.sum(sel * spread, axis=1, keepdims=True)
-        r0 = routes_ref[t, :, 0:1]
-        r1 = routes_ref[t, :, 1:2]
+        r0 = route_col(t, 0)
+        r1 = route_col(t, 1)
         named_b = ((r0 == slot_eb) | (r1 == slot_eb)).astype(F32)
         before_b = dot(lower, named_b.astype(BF16), ((1,), (0,)))
         selb_s[t] = jnp.where(before_b == slot_cb.astype(F32), named_b, 0.0).astype(BF16)
         return carry
 
+    loads[0].wait()
     lax.fori_loop(0, MICRO, prepare, 0)
+    for cp in loads[1:]:
+        cp.wait()
 
     def dispatch(t):
         @pl.when(t >= 2)
@@ -284,14 +309,14 @@
         scores = jnp.zeros((TOK, 2 * TOK), F32)
         for q in range(4):
             cols = slice(q * QB, (q + 1) * QB)
-            scores += dot(UP[t, :, cols], eo_ref[t, :, cols], ((1,), (1,)))
+            scores += dot(UP[t, :, cols], eo_ref[t, :, :, cols].reshape(2 * TOK, QB), ((1,), (1,)))
         row_i = iota((TOK, 2 * TOK), 0)
         col_i = iota((TOK, 2 * TOK), 1)
         s0 = jnp.sum(jnp.where(col_i == 2 * row_i, scores, 0.0), axis=1, keepdims=True)
         s1 = jnp.sum(jnp.where(col_i == 2 * row_i + 1, scores, 0.0), axis=1, keepdims=True)
         expert_i = iota((TOK, EXPERTS), 1)
-        prob_grad = jnp.where(routes_ref[t, :, 0:1] == expert_i, s0, 0.0) + jnp.where(
-            routes_ref[t, :, 1:2] == expert_i, s1, 0.0
+        prob_grad = jnp.where(route_col(t, 0) == expert_i, s0, 0.0) + jnp.where(
+            route_col(t, 1) == expert_i, s1, 0.0
         )
         probs = probs_s[t]
         logit_grad = (
@@ -540,40 +565,55 @@
     t0(0)
     grads_a()
 
-    def step(s, carry):
-        for lag, fn in ((0, t0), (3, t3), (2, t2), (1, t1), (5, r1), (6, r2), (4, t4)):
-            low = lag + (1 if fn is t0 else 0)
-
-            @pl.when((s >= low) & (s < CHUNKS + lag))
-            def _():
-                fn(s - lag)
-
-        @pl.when(s == 1)
-        def _():
-            dispatch_relay(2)
-
-        for when, fn in ((2, grads_b), (5, grads_c), (8, grads_d)):
-
-            @pl.when(s == when)
-            def _():
-                fn()
-
-        return carry
-
-    lax.fori_loop(0, CHUNKS + 7, step, 0)
-
-    for t in range(MICRO):
-        gate_f = gate_ref[t].astype(F32)
-        sig = jax.nn.sigmoid(gate_f)
-        rows = inner[t]
-        stage[0, t] = (rows * gate_f * sig).astype(BF16)
-        stage[1, t] = (rows * scan_ref[t].astype(F32) * sig * (1.0 + gate_f * (1.0 - sig))).astype(BF16)
     fin = [
         pltpu.make_async_copy(stage.at[0], scan_out, fin_sem.at[0]),
         pltpu.make_async_copy(stage.at[1], gate_out, fin_sem.at[1]),
     ]
-    for cp in fin:
-        cp.start()
+
+    def finish_mixer():
+        for t in range(MICRO):
+            gate_f = gate_ref[t].astype(F32)
+            sig = jax.nn.sigmoid(gate_f)
+            rows = inner[t]
+            stage[0, t] = (rows * gate_f * sig).astype(BF16)
+            stage[1, t] = (rows * scan_ref[t].astype(F32) * sig * (1.0 + gate_f * (1.0 - sig))).astype(BF16)
+        for cp in fin:
+            cp.start()
+
+    def dx_copy(t):
+        return pltpu.make_async_copy(DX.at[t], exp_out.at[t], dx_sem.at[t])
+
+    def step(s, carry):
+        for lag, fn in ((0, t0), (3, t3), (2, t2), (1, t1), (5, r1), (6, r2), (4, t4)):
+            low = lag + (1 if fn is t0 else 0)
+
+            @pl.when((s >= low) & (s < CHUNKS + lag))
+            def _():
+                fn(s - lag)
+
+        @pl.when(s == 1)
+        def _():
+            dispatch_relay(2)
+
+        for when, fn in ((2, grads_b), (5, grads_c), (8, grads_d)):
+
+            @pl.when(s == when)
+            def _():
+                fn()
+
+        @pl.when(s == CHUNKS + 4)
+        def _():
+            finish_mixer()
+
+        return carry
+
+    lax.fori_loop(0, CHUNKS + 6, step, 0)
+    for t in range(MICRO):
+        for k in range(1, 4):
+            d2_copy(t, k, True).wait_recv()
+        if t >= 1:
+            d2_local(t).wait()
+        dx_copy(t).start()
 
     def drain(c, carry):
         for h in range(2):
@@ -591,7 +631,6 @@
     def drain_t(t, carry):
         for k in range(1, 4):
             b1_copy(t, k, False).wait_send()
-            d2_copy(t, k, True).wait_recv()
         po_copy(t).wait()
         return carry
 
@@ -601,7 +640,6 @@
             b2_copy(t, k, False).wait_send()
             d1_copy(t, k, False).wait_send()
             d2_copy(t, k, False).wait_send()
-        d2_local(t).wait()
 
     @pl.when(sec == 1)
     def _():
@@ -615,10 +653,12 @@
     each_peer(lambda k: rc_copy(k, False).wait_send())
     for cp in fin:
         cp.wait()
+    for t in range(MICRO):
+        dx_copy(t).wait()
     rg_fin.wait()
 
 
-def layer(inc, hid, eo, routes, routes_t, back, scan, gate, weight, rg):
+def layer(inc, hid, eo, routes_t, back, scan, gate, weight, router, gain):
     vmem = pl.BlockSpec(memory_space=pltpu.VMEM)
     hbm = pl.BlockSpec(memory_space=pl.ANY)
     V = pltpu.VMEM
@@ -633,7 +673,7 @@
             jax.ShapeDtypeStruct((512, QB), F32),
             jax.ShapeDtypeStruct((24, QB), F32),
         ),
-        in_specs=[hbm, vmem, vmem, vmem, vmem, hbm, vmem, vmem, hbm, vmem],
+        in_specs=[hbm, hbm, hbm, vmem, hbm, hbm, hbm, hbm, vmem, vmem],
         out_specs=(hbm,) * 6,
         scratch_shapes=[
             V((CHUNKS, MICRO, 4, 64, CCOL), BF16),
@@ -663,6 +703,15 @@
             V((2, SLOTS, WIDTH), BF16),
             V((MICRO, SLOTS, WIDTH), BF16),
             V((2, SLOTS, WIDTH), BF16),
+            V((MICRO, TOK, WIDTH), BF16),
+            V((MICRO, TOK, 2, WIDTH), BF16),
+            V((MICRO, 256, 512), BF16),
+            V((MICRO, 256, 512), BF16),
+            DMA((4,)),
+            V((MICRO, SLOTS, WIDTH), BF16),
+            V((MICRO, SLOTS, WIDTH), BF16),
+            DMA((MICRO,)),
+            DMA((MICRO,)),
             V((MICRO, TOK, EXPERTS), F32),
             V((MICRO, SLOTS, 1), F32),
             V((MICRO, SLOTS, TOK), BF16),
@@ -688,28 +737,57 @@
             collective_id=0, has_side_effects=True, vmem_limit_bytes=63 * 1024 * 1024
         ),
         cost_estimate=pl.CostEstimate(flops=14_000_000_000, bytes_accessed=30_000_000, transcendentals=0),
-    )(inc, hid, eo, routes, routes_t, back, scan, gate, weight, rg)
+    )(inc, hid, eo, routes_t, back, scan, gate, weight, router, gain)
+
+
+def finish_kernel(*refs):
+    small, router, gain = refs[5], refs[11], refs[12]
+    stages, sems = refs[13:18], refs[18]
+    loads = [pltpu.make_async_copy(refs[n], stages[n], sems.at[0, n]) for n in range(5)]
+    stores = [pltpu.make_async_copy(stages[n], refs[6 + n], sems.at[1, n]) for n in range(5)]
+    for cp in loads:
+        cp.start()
+    router[...] = small[0:EXPERTS, :]
+    gain[...] = small[EXPERTS : EXPERTS + 1, :]
+    for load, store in zip(loads, stores):
+        load.wait()
+        store.start()
+    for cp in stores:
+        cp.wait()
+
+
+def finish(arrays):
+    vmem = pl.BlockSpec(memory_space=pltpu.VMEM)
+    hbm = pl.BlockSpec(memory_space=pl.ANY)
+    return pl.pallas_call(
+        finish_kernel,
+        out_shape=tuple(jax.ShapeDtypeStruct(a.shape, a.dtype) for a in arrays[:5])
+        + (jax.ShapeDtypeStruct((EXPERTS, QB), F32), jax.ShapeDtypeStruct((1, QB), F32)),
+        in_specs=[hbm] * 5 + [vmem],
+        out_specs=(hbm,) * 5 + (vmem, vmem),
+        scratch_shapes=[pltpu.VMEM(a.shape, a.dtype) for a in arrays[:5]]
+        + [pltpu.SemaphoreType.DMA((2, 5))],
+        compiler_params=pltpu.CompilerParams(vmem_limit_bytes=32 * 1024 * 1024),
+        cost_estimate=pl.CostEstimate(flops=0, bytes_accessed=20_000_000, transcendentals=0),
+    )(*arrays)
 
 
 def on_device(
     incoming, hidden, expert_out, routes, expert_back, scan_out, gate_in, w_out, w_router, norm_gain
 ):
-    rg = jnp.concatenate(
-        [w_router[0].T, norm_gain, jnp.zeros((15, w_router.shape[1]), w_router.dtype)], axis=0
+    outs = layer(
+        incoming[0], hidden[0], expert_out[0], jnp.swapaxes(routes[0], 1, 2), expert_back[0],
+        scan_out[0], gate_in[0], w_out[0], w_router[0].T, norm_gain,
     )
-    eo = expert_out[0].reshape(MICRO, 2 * TOK, WIDTH)
-    passed, scan_grad, gate_grad, expert_grad, weight_grad, small = layer(
-        incoming[0], hidden[0], eo, routes[0], jnp.swapaxes(routes[0], 1, 2), expert_back[0],
-        scan_out[0], gate_in[0], w_out[0], rg,
-    )
+    passed, scan_grad, gate_grad, expert_grad, weight_grad, router, gain = finish(outs)
     return (
         passed[None],
         scan_grad[None],
         gate_grad[None],
         expert_grad[None],
         weight_grad[None],
-        small[:EXPERTS].T[None],
-        small[EXPERTS : EXPERTS + 1],
+        router.T[None],
+        gain,
     )
 
 

time: 221 us -> 212 us (0.959)
  local copies, waits for them, and re-layouts: 19.8 us -> 8.39 us
  Pallas kernels: 199 us -> 202 us
    pallas_call x0 -> x1, Pallas kernels: none -> 5.23 us  [finish(): pl.pallas_call(finish_kernel, out_shape=tuple((jax.ShapeDtypeStruct(a.sha...]
    another operation x1 -> x0, local copies, waits for them, and re-layouts: 3.63 us -> none  [on_device(): eo = expert_out[0].reshape(MICRO, 2 * TOK, WIDTH)]
    unnamed x9 -> x12, local copies, waits for them, and re-layouts: 11.5 us -> 8.39 us
where the time goes in v3:
time: 212 us; the launch traced here: 211 us
  Pallas kernels  202 us (95%)
  local copies, waits for them, and re-layouts  8.39 us (4%)
    pallas_call x1, Pallas kernels, layer(): pl.pallas_call(layer_kernel, out_shape=(jax.ShapeDtypeStruct((MICRO, TOK,...  197 us
    unnamed x12, local copies, waits for them, and re-layouts  8.39 us
    pallas_call x1, Pallas kernels, finish(): pl.pallas_call(finish_kernel, out_shape=tuple((jax.ShapeDtypeStruct(a.sha...  5.23 us

profile of v3, /device:TPU:1, one launch (start us, length us, event | category | flops | bytes accessed | tf_op | source)
XLA Modules:
  0.0 211.2 jit_solution(13716302596011252283)
XLA Ops:
  0.6 196.9 %shard_map.153 = (bf16[3,16,8192]{2,1,0:T(8,128)(2,1)}, bf16[3,256,512]{2,1,0:T(8,128)(2,1)}, bf16[3,256,512]{2,1,0:T(8,128)(2,1)}, bf16[3,64,8192]{2,1,0:T(8,12...) custom-call(bf16[3,16,8192]{2,1,0:T(8,128)(2,1)} %bitcast.26, bf16[3,16,8192]{2,1,0:T(8,128)(2,1)} %bitcast.27, ...), custom_call_target="tpu_custom_call" | custom-call | flops 14000000000 | bytes 30000000 | tf_op jit(solution)/shard_map/pallas_call | solution.py:666
  197.6 0.0 copy-start
  197.6 2.2 %copy-done = f32[512,2048]{1,0:T(8,128)S(1)} copy-done((f32[512,2048]{1,0:T(8,128)S(1)}, f32[512,2048]{1,0:T(8,128)}, u32[]{:S(2)}) %copy-start) | copy-done | bytes 4194328
  199.8 0.0 copy-start.1
  199.8 1.9 copy-done.1
  201.7 0.0 copy-start.2
  201.7 1.1 copy-done.2
  202.8 0.0 copy-start.3
  202.8 1.1 copy-done.3
  203.9 0.0 copy-start.4
  203.9 1.1 copy-done.4
  205.1 0.0 copy-start.5
  205.1 0.9 copy-done.5
  206.0 5.2 %shard_map.154 = (bf16[3,16,8192]{2,1,0:T(8,128)(2,1)}, bf16[3,256,512]{2,1,0:T(8,128)(2,1)}, bf16[3,256,512]{2,1,0:T(8,128)(2,1)}, bf16[3,64,8192]{2,1,0:T(8,12...) custom-call(bf16[3,16,8192]{2,1,0:T(8,128)(2,1)S(1)} %copy-done.2, ...), custom_call_target="tpu_custom_call" | custom-call | bytes 20000000 | tf_op jit(solution)/shard_map/pallas_call | solution.py:762
Async XLA Ops:
  197.6 2.2 %copy-start = (f32[512,2048]{1,0:T(8,128)S(1)}, f32[512,2048]{1,0:T(8,128)}, u32[]{:S(2)}) copy-start(f32[512,2048]{1,0:T(8,128)} %get-tuple-element.24.refs_4_) | copy-start | bytes 12582916
  199.8 1.9 copy-start.1
  201.7 1.1 copy-start.2
  202.8 1.1 copy-start.3
  203.9 1.1 copy-start.4
  205.1 0.9 copy-start.5

commit v4 on v3

--- a/solution.py
+++ b/solution.py
@@ -767,7 +767,7 @@
         out_specs=(hbm,) * 5 + (vmem, vmem),
         scratch_shapes=[pltpu.VMEM(a.shape, a.dtype) for a in arrays[:5]]
         + [pltpu.SemaphoreType.DMA((2, 5))],
-        compiler_params=pltpu.CompilerParams(vmem_limit_bytes=32 * 1024 * 1024),
+        compiler_params=pltpu.CompilerParams(vmem_limit_bytes=62 * 1024 * 1024),
         cost_estimate=pl.CostEstimate(flops=0, bytes_accessed=20_000_000, transcendentals=0),
     )(*arrays)
 

time: 212 us -> 207 us (0.976)
  local copies, waits for them, and re-layouts: 8.39 us -> 0 us
  Pallas kernels: 202 us -> 206 us
    unnamed x12 -> x0, local copies, waits for them, and re-layouts: 8.39 us -> none
    pallas_call x1, Pallas kernels: 5.23 us -> 8.88 us  [finish(): pl.pallas_call(finish_kernel, out_shape=tuple((jax.ShapeDtypeStruct(a.sha...]
where the time goes in v4:
time: 207 us; the launch traced here: 206 us
  Pallas kernels  206 us (100%)
    pallas_call x1, Pallas kernels, layer(): pl.pallas_call(layer_kernel, out_shape=(jax.ShapeDtypeStruct((MICRO, TOK,...  197 us
    pallas_call x1, Pallas kernels, finish(): pl.pallas_call(finish_kernel, out_shape=tuple((jax.ShapeDtypeStruct(a.sha...  8.88 us

profile of v4, /device:TPU:1, one launch (start us, length us, event | category | flops | bytes accessed | tf_op | source)
XLA Modules:
  0.0 206.5 jit_solution(9451728497743751160)
XLA Ops:
  0.6 196.9 %shard_map.153 = (bf16[3,16,8192]{2,1,0:T(8,128)(2,1)}, bf16[3,256,512]{2,1,0:T(8,128)(2,1)}, bf16[3,256,512]{2,1,0:T(8,128)(2,1)}, bf16[3,64,8192]{2,1,0:T(8,12...) custom-call(bf16[3,16,8192]{2,1,0:T(8,128)(2,1)} %bitcast.26, bf16[3,16,8192]{2,1,0:T(8,128)(2,1)} %bitcast.27, ...), custom_call_target="tpu_custom_call" | custom-call | flops 14000000000 | bytes 30000000 | tf_op jit(solution)/shard_map/pallas_call | solution.py:666
  197.6 8.9 %shard_map.154 = (bf16[3,16,8192]{2,1,0:T(8,128)(2,1)}, bf16[3,256,512]{2,1,0:T(8,128)(2,1)}, bf16[3,256,512]{2,1,0:T(8,128)(2,1)}, bf16[3,64,8192]{2,1,0:T(8,12...) custom-call(bf16[3,16,8192]{2,1,0:T(8,128)(2,1)} %get-tuple-element.20.refs_0_, ...), custom_call_target="tpu_custom_call" | custom-call | bytes 20000000 | tf_op jit(solution)/shard_map/pallas_call | solution.py:762
